TPU v7x, 32 devices: a whole 2x2x4 slice. The times are simulated.
32 devices in a mesh: mod: 4 (over y, x), blk: 8 (over z, core).
Axes of the slice: x: 2, y: 2, z: 4, core: 2. Of those that a mesh axis runs over, the one named last changes fastest.
Arguments:
- intensity: bfloat16 [32768, 1024], P('mod', 'blk'), may hold values from 0.1 to 810
- pixel_bin: int32 [32768], replicated, may hold values from 0 to 199, as said below
Outputs:
- two_time: float32 [200, 32, 32], P('mod', 'blk')
Inputs may be any that keep to these rules, and one draw needn't show every extreme that they name: `pixel_bin`: owner o holds the bins o * 50 to (o + 1) * 50 - 1. Of the 8192 pixels of one module group (an aligned block of entries), at most 4096 lie in the bins of one owner, and in every draw some owner receives exactly 4096 from every module group. Every bin holds at least one pixel.
All inputs are finite; a program needn't handle non-finite values.
Results may differ from a plain program's by a relative error of at most 0.0007.
Values may be sent and summed in bfloat16 or wider, within the bound.
No kernel may reach another device: no remote copies, remote signals or barrier semaphores. Data moves between devices by JAX's collectives and lax.ppermute only.
A program may use at most 128 MiB of HBM per device.

v0:
```python
import jax
import jax.numpy as jnp
from jax import lax
from jax.sharding import PartitionSpec as P

NBINS = 200
TBIN = 4


def first_members(selected, slot_size):
    width = selected.shape[1]
    position = jnp.arange(width, dtype=jnp.int32)[None, :]
    sort_keys = jnp.where(selected, position, width + position)
    order = jnp.argsort(sort_keys, axis=1, stable=True)[:, :slot_size]
    member_count = jnp.sum(selected.astype(jnp.int32), axis=1, keepdims=True)
    valid = jnp.arange(slot_size, dtype=jnp.int32)[None, :] < member_count
    return (order, valid)


def pool_matrix(frame_count, time_bins):
    pool_size = frame_count // time_bins
    frame_ids = jnp.arange(frame_count, dtype=jnp.int32)[:, None] // pool_size
    columns = jnp.arange(time_bins, dtype=jnp.int32)[None, :]
    return jnp.where(frame_ids == columns, 1.0 / pool_size, 0.0).astype(jnp.float32)


def body(intensity, pixel_bin):
    module_count = lax.axis_size("mod")
    module = lax.axis_index("mod")
    pix_local, frame_count = intensity.shape
    slot_size = pix_local // 2
    bins_owned = NBINS // module_count
    time_bins = TBIN
    slot_total = module_count * slot_size
    highest = lax.Precision.HIGHEST
    pooling = pool_matrix(frame_count, time_bins)
    all_bins = pixel_bin.reshape(module_count, pix_local)
    is_mine = all_bins // bins_owned == module
    mine_order, mine_valid = first_members(is_mine, slot_size)
    arrived_bins = jnp.take_along_axis(all_bins, mine_order, axis=1) - module * bins_owned
    arrived = jnp.where(mine_valid, arrived_bins, bins_owned).reshape(slot_total)
    bin_ids = jnp.arange(bins_owned, dtype=jnp.int32)[None, :]
    owner_onehot = (arrived[:, None] == bin_ids).astype(jnp.bfloat16)
    own_counts = jnp.sum(owner_onehot, axis=0, dtype=jnp.float32)
    local_bins = lax.dynamic_slice_in_dim(pixel_bin, module * pix_local, pix_local)
    destination = local_bins // bins_owned
    to_each = destination[None, :] == jnp.arange(module_count, dtype=jnp.int32)[:, None]
    send_order, send_valid = first_members(to_each, slot_size)
    source_rows = jnp.where(send_valid, send_order, pix_local).reshape(slot_total)
    outgoing = jnp.take(intensity, source_rows, axis=0, mode="fill", fill_value=0)
    received = lax.all_to_all(outgoing, "mod", split_axis=0, concat_axis=0, tiled=True)
    totals = lax.dot_general(
        owner_onehot, received, (((0,), (0,)), ((), ())), preferred_element_type=jnp.float32
    )
    bin_means = totals / jnp.maximum(own_counts, 1.0)[:, None]
    onehot_wide = (arrived[:, None] == bin_ids).astype(jnp.float32)
    has_bin = jnp.sum(onehot_wide, axis=1, keepdims=True)
    row_means = jnp.dot(onehot_wide, bin_means, precision=highest) + (1.0 - has_bin)
    ratios = received.astype(jnp.float32) / row_means
    pooled = lax.dot_general(pooling, ratios, (((0,), (1,)), ((), ())), precision=highest).astype(
        jnp.bfloat16
    )
    expanded = (owner_onehot[:, :, None] * pooled.T[:, None, :]).reshape(
        slot_total, bins_owned * time_bins
    )
    piece = lax.all_gather(pooled, "blk", axis=0, tiled=True)
    column_count = piece.shape[0]
    result = lax.dot_general(
        expanded, piece, (((0,), (1,)), ((), ())), preferred_element_type=jnp.float32
    )
    gram_rows = result.reshape(bins_owned, time_bins, column_count)
    return gram_rows / jnp.maximum(own_counts, 1.0)[:, None, None]


def solution(mesh):
    in_specs = (P("mod", "blk"), P())
    out_specs = P("mod", "blk", None)
    return jax.shard_map(body, mesh=mesh, in_specs=in_specs, out_specs=out_specs, check_vma=False)
```

profile of v0, /device:TPU:0, one launch (start us, length us, event | category | flops | bytes accessed | tf_op | source)
XLA Modules:
  0.0 321.0 jit_solution(4711384653366112195)
XLA Ops:
  6.5 1.1 reshape.170
  7.6 0.8 add_select_fusion.1
  8.4 0.3 convert_reduce_fusion.3
  8.8 0.9 iota_select_fusion.1
  9.7 0.7 iota.51
  10.4 0.7 iota.49
  11.1 27.0 %sort.32.cloned.1.call-done = (s32[4,8192]{1,0:T(4,128)}, s32[4,8192]{1,0:T(4,128)}) async-done(((s32[4,8192]{1,0:T(4,128)}, s32[4,8192]{1,0:T(4,128)}), (s32[4,8192]{1,0:T(4,128)}, s32[4,8192]{1,0:T(4,128)})) %sort.32.cloned.1.call-update) | async-done | bytes 262160 | tf_op jit(solution)/shard_map/jit(argsort)/sort | solution.py:14
  38.1 0.9 fusion.15
  39.0 1.0 compare_and_fusion
  40.2 57.4 %gather_fusion = bf16[16384,128]{1,0:T(8,128)(2,1)} fusion(bf16[8192,128]{1,0:T(8,128)(2,1)S(1)} %copy-done, s32[16384]{0:T(1024)S(1)} %broadcast_clamp_fusion), kind=kCustom, calls=%fused_computation | custom fusion | bytes 8454144 | tf_op jit(solution)/shard_map/jit(_take)/gather | solution.py:50
  97.6 8.9 %broadcast_select_fusion = bf16[4,4096,128]{2,1,0:T(8,128)(2,1)} fusion(bf16[4,4096,128]{2,1,0:T(8,128)(2,1)} %bitcast.30, pred[4,4096]{1,0:T(4,128)(4,1)S(1)} %compare_and_fusion), kind=kLoop, calls=%fused_computation.7 | loop fusion | flops 2097152 | bytes 8404992 | tf_op jit(solution)/shard_map/jit(_take)/select_n | solution.py:50
  106.4 5.2 %all-to-all-start = ((bf16[4,4096,128]{2,1,0:T(8,128)(2,1)}), bf16[4,4096,128]{2,1,0:T(8,128)(2,1)}, u32[]{:S(2)}, u32[]{:S(2)}) async-start(bf16[4,4096,128]{2,1,0:T(8,128)(2,1)} %broadcast_select_fusion), calls=%async_computation | async-start | bytes 8388608 | tf_op jit(solution)/shard_map/all_to_all | solution.py:51
  111.6 0.9 fusion.13
  112.5 138.1 %gather_fusion.1 = s32[16384]{0:T(1024)S(1)} fusion(s32[4,8192]{1,0:T(4,128)S(1)} %reshape.170, s32[16384]{0:T(1024)S(1)} %bitcast.28), kind=kCustom, calls=%fused_computation.1 | custom fusion | bytes 262144 | tf_op jit(solution)/shard_map/jit(take_along_axis)/gather | solution.py:40
  250.7 0.7 convert_reduce_fusion
  251.5 1.6 fusion.4
  253.1 2.9 fusion.7
  256.0 10.7 %fusion = f32[16384,128]{1,0:T(8,128)S(1)} fusion(f32[50,128]{1,0:T(8,128)S(1)} %fusion.7, bf16[16384,128]{1,0:T(8,128)(2,1)} %bitcast.3, f32[16384]{0:T(1024)S(1)} %broadcast_subtract_fusion, s32[16384]{0:T(1024)S(1)} %bitcast.36), kind=kOutput, calls=%fused_computation.4 | convolution fusion | flops 1265401856 | bytes 12739584 | tf_op jit(solution)/shard_map/dot_general | solution.py:58
  266.7 7.8 %convolution_convert_fusion = bf16[4,16384]{1,0:T(4,128)(2,1)} fusion(f32[16384,128]{1,0:T(8,128)S(1)} %fusion, s32[128]{0:T(128)S(1)} %and_select_fusion), kind=kOutput, calls=%fused_computation.3 | convolution fusion | flops 100729856 | bytes 8520192 | tf_op jit(solution)/shard_map/dot_general | solution.py:60
  274.5 7.4 %broadcast_multiply_fusion = bf16[16384,50,4]{0,2,1:T(4,128)(2,1)} fusion(bf16[16384,4]{0,1:T(4,128)(2,1)} %bitcast.32, bf16[16384,50]{0,1:T(8,128)(2,1)} %fusion.4), kind=kLoop, calls=%fused_computation.13 | loop fusion | flops 3276800 | bytes 8323072 | tf_op jit(solution)/shard_map/mul | solution.py:63
  281.9 11.4 %mul.28 = bf16[16384,200]{0,1:T(8,128)(2,1)} reshape(bf16[16384,50,4]{0,2,1:T(4,128)(2,1)} %broadcast_multiply_fusion) | data formatting | bytes 13107200 | tf_op jit(solution)/shard_map/mul | solution.py:63
  293.4 11.9 %dot_general.20 = bf16[50,4,16384]{2,1,0:T(4,128)(2,1)} reshape(bf16[200,16384]{1,0:T(8,128)(2,1)} %bitcast.29) | data formatting | bytes 13107200 | tf_op jit(solution)/shard_map/dot_general | solution.py:68
  305.3 1.5 reshape.194
  306.8 7.6 %fusion.8 = f32[50,4,32]{0,2,1:T(8,128)} fusion(bf16[32,16384,1]{1,0,2:T(8,128)(2,1)S(1)} %reshape.194, bf16[50,4,16384]{2,1,0:T(4,128)(2,1)} %dot_general.20, f32[50]{0:T(128)S(1)} %broadcast_maximum_fusion), kind=kOutput, calls=%fused_computation.17 | convolution fusion | flops 209721600 | bytes 7627976 | tf_op jit(solution)/shard_map/dot_general | solution.py:68
  (23 shorter events, 0.4 us)
Async XLA Ops:
  6.5 33.6 %copy-start = (bf16[8192,128]{1,0:T(8,128)(2,1)S(1)}, bf16[8192,128]{1,0:T(8,128)(2,1)}, u32[]{:S(2)}) copy-start(bf16[8192,128]{1,0:T(8,128)(2,1)} %param.2) | copy-start | bytes 6291460
  6.5 31.6 %sort.32.cloned.1.call-start = ((), (), s32[]{:S(2)}) async-start(), calls=%async_computation.3 | async-start | bytes 786464 | tf_op jit(solution)/shard_map/jit(argsort)/sort | solution.py:14
  10.4 101.2 %sort.30.cloned.1.call-start = ((), (), s32[]{:S(2)}) async-start(), calls=%async_computation.2 | async-start | bytes 786464 | tf_op jit(solution)/shard_map/jit(argsort)/sort | solution.py:14
  106.4 146.7 %all-to-all-start = ((bf16[4,4096,128]{2,1,0:T(8,128)(2,1)}), bf16[4,4096,128]{2,1,0:T(8,128)(2,1)}, u32[]{:S(2)}, u32[]{:S(2)}) async-start(bf16[4,4096,128]{2,1,0:T(8,128)(2,1)} %broadcast_select_fusion), calls=%async_computation | async-start | bytes 8388608 | tf_op jit(solution)/shard_map/all_to_all | solution.py:51
  111.6 193.7 %all-gather.3.cloned.1.call-start = ((), (), s32[]{:S(2)}) async-start(), calls=%async_computation.1 | async-start | bytes 1179648 | tf_op jit(solution)/shard_map/all_gather | solution.py:66
  112.5 138.2 %copy-start.1 = (s32[4,8192]{1,0:T(4,128)S(1)}, s32[4,8192]{1,0:T(4,128)}, u32[]{:S(2)}) copy-start(s32[4,8192]{1,0:T(4,128)} %get-tuple-element.7) | copy-start | bytes 393220
Sparse Core Ops, SparseCore 0:
  10.5 27.3 sort.36.cloned.1.call-done
  40.6 27.3 sort.34.cloned.1.call-done
  274.6 24.9 all-gather.2
  (2 shorter events, 0.0 us)
where the time goes:
time: 323 us; the launch traced here: 321 us
  local copies, waits for them, and re-layouts  250 us (77%)
  matrix products  29 us (9%)
  other arithmetic  23.6 us (7%)
  between operations  13.2 us (4%)
  starting transfers between devices  5.15 us (2%)
    gather x2, local copies, waits for them, and re-layouts, body(): jnp.take_along_axis(all_bins, mine_order, axis=1) - module * bins_owned  138 us
    gather x1, local copies, waits for them, and re-layouts, body(): jnp.take(intensity, source_rows, axis=0, mode='fill', fill_value=0)  57.4 us
    sort x4, local copies, waits for them, and re-layouts, first_members(): order = jnp.argsort(sort_keys, axis=1, stable=True)[:, :slot_size]  27 us
    dot_general x1, local copies, waits for them, and re-layouts, body(): lax.dot_general(expanded, piece, (((0,), (1,)), ((), ())), preferred_elem...  11.9 us
    mul x1, local copies, waits for them, and re-layouts, body(): owner_onehot[:, :, None] * pooled.T[:, None, :]  11.4 us
    dot_general x1, matrix products, body(): jnp.dot(onehot_wide, bin_means, precision=highest) + (1.0 - has_bin)  10.7 us
    select_n x2, other arithmetic, body(): jnp.take(intensity, source_rows, axis=0, mode='fill', fill_value=0)  8.92 us
    dot_general x1, matrix products, body(): lax.dot_general(pooling, ratios, (((0,), (1,)), ((), ())), precision=high...  7.78 us
  transfers between devices with their start and end apart: 2, of which 0 were waited for; matrix products, arithmetic and copies ran while one was open for 54% of the time, Pallas kernels for 0%

commit v1 on v0

v1 whole, which is shorter than its diff:
```python
import functools

import jax
import jax.numpy as jnp
from jax import lax
from jax.experimental import pallas as pl
from jax.experimental.pallas import tpu as pltpu
from jax.sharding import PartitionSpec as P

NBINS = 200
TBIN = 4
F32 = jnp.float32
BF16 = jnp.bfloat16
NT = (((1,), (1,)), ((), ()))
TN = (((0,), (0,)), ((), ()))


def round_up(value, multiple):
    return (value + multiple - 1) // multiple * multiple


def onehot_rows(index_row, rows):
    row_ids = lax.broadcasted_iota(jnp.int32, (rows, index_row.shape[1]), 0)
    return jnp.where(row_ids == index_row, 1.0, 0.0).astype(BF16)


def split_hi_lo(value):
    hi = value.astype(BF16)
    lo = (value - hi.astype(F32)).astype(BF16)
    return hi, lo


def totals_kernel(bins_ref, intensity_ref, out_ref, *, chunk):
    rows, _ = out_ref.shape
    acc = jnp.zeros(out_ref.shape, F32)
    for start in range(0, bins_ref.shape[1], chunk):
        onehot = onehot_rows(bins_ref[:, start : start + chunk], rows)
        acc += jnp.dot(onehot, intensity_ref[start : start + chunk, :], preferred_element_type=F32)
    out_ref[...] = acc


def prepare_kernel(bins_ref, intensity_ref, counts_ref, flipped_ref, *, chunk):
    rows, lanes = counts_ref.shape
    frames = intensity_ref.shape[1]
    eye = (
        lax.broadcasted_iota(jnp.int32, (frames, frames), 0)
        == lax.broadcasted_iota(jnp.int32, (frames, frames), 1)
    )
    eye = jnp.where(eye, 1.0, 0.0).astype(BF16)
    for start in range(0, intensity_ref.shape[0], chunk):
        block = intensity_ref[start : start + chunk, :]
        flipped = lax.dot_general(eye, block, NT, preferred_element_type=F32)
        flipped_ref[:, start : start + chunk] = flipped.astype(BF16)
    row_ids = lax.broadcasted_iota(jnp.int32, (rows, lanes), 0)

    def step(k, acc):
        piece = bins_ref[:, pl.ds(pl.multiple_of(k * 8 * lanes, 8 * lanes), 8 * lanes)]
        for s in range(8):
            acc += jnp.where(row_ids == piece[:, s * lanes : (s + 1) * lanes], 1.0, 0.0)
        return acc

    acc = lax.fori_loop(0, bins_ref.shape[1] // (8 * lanes), step, jnp.zeros((rows, lanes), F32))
    counts_ref[...] = jnp.broadcast_to(jnp.sum(acc, axis=1, keepdims=True), (rows, lanes))


def pool_kernel(bins_ref, counts_ref, flipped_ref, own_ref, *rest, chunk):
    *other_refs, out_ref = rest
    rows, frames = own_ref.shape
    totals = own_ref[...]
    for other in other_refs:
        totals += other[...]
    pool = frames // out_ref.shape[0]
    counts = counts_ref[...]
    weights = counts / (jnp.where(counts > 0.0, totals, 1.0) * float(pool))
    hi, lo = split_hi_lo(weights)
    both = jnp.concatenate([hi, lo], axis=1)
    for start in range(0, bins_ref.shape[1], chunk):
        onehot = onehot_rows(bins_ref[:, start : start + chunk], rows)
        spread = lax.dot_general(both, onehot, TN, preferred_element_type=F32)
        spread = spread[:frames, :] + spread[frames:, :]
        ratios = flipped_ref[:, start : start + chunk].astype(F32) * spread
        pooled = [
            jnp.sum(ratios[i * pool : (i + 1) * pool, :], axis=0, keepdims=True)
            for i in range(out_ref.shape[0])
        ]
        out_ref[:, start : start + chunk] = jnp.concatenate(pooled, axis=0).astype(BF16)


def gram_kernel(index_ref, own_ref, all_ref, out_ref, *, chunk):
    rows = out_ref.shape[0]
    tbin = own_ref.shape[0]
    cols = all_ref.shape[0]
    width = tbin * cols
    acc = jnp.zeros((rows, 2 * width), F32)
    for start in range(0, index_ref.shape[1], chunk):
        onehot = onehot_rows(index_ref[:, start : start + chunk], rows)
        own = own_ref[:, start : start + chunk].astype(F32)
        every = all_ref[:, start : start + chunk].astype(F32)
        his, los = [], []
        for i in range(tbin):
            hi, lo = split_hi_lo(own[i : i + 1, :] * every)
            his.append(hi)
            los.append(lo)
        products = jnp.concatenate(his + los, axis=0)
        acc += lax.dot_general(onehot, products, NT, preferred_element_type=F32)
    out_ref[...] = acc[:, :width] + acc[:, width:]


def call(kernel, out_shape, *args, flops, limit=48 << 20):
    vmem = pl.BlockSpec(memory_space=pltpu.VMEM)
    shapes = out_shape if isinstance(out_shape, tuple) else (out_shape,)
    moved = sum(a.size * a.dtype.itemsize for a in args)
    moved += sum(s.size * s.dtype.itemsize for s in shapes)
    return pl.pallas_call(
        kernel,
        out_shape=out_shape,
        in_specs=[vmem] * len(args),
        out_specs=(vmem,) * len(shapes) if isinstance(out_shape, tuple) else vmem,
        compiler_params=pltpu.CompilerParams(vmem_limit_bytes=limit),
        cost_estimate=pl.CostEstimate(flops=flops, bytes_accessed=moved, transcendentals=0),
    )(*args)


def swap(value, axis, distance):
    size = lax.axis_size(axis)
    return lax.ppermute(value, axis, [(i, i ^ distance) for i in range(size)])


def gather_blocks(pooled):
    n_blk = lax.axis_size("blk")
    if n_blk > 8 or n_blk % 2:
        return lax.all_gather(pooled, "blk", axis=0, tiled=True)
    k = lax.axis_index("blk")
    same_core = [pooled] + [swap(pooled, "blk", 2 * s) for s in range(1, n_blk // 2)]
    mine = jnp.stack(same_core)
    sibling = swap(mine, "blk", 1)
    pairs = jnp.stack([mine, sibling], axis=1)
    flat = pairs.reshape((n_blk,) + pooled.shape)
    order = jnp.arange(n_blk, dtype=jnp.int32) ^ k
    return flat[order].reshape(n_blk * pooled.shape[0], pooled.shape[1])


def body(intensity, pixel_bin):
    n_mod = lax.axis_size("mod")
    n_blk = lax.axis_size("blk")
    module = lax.axis_index("mod")
    pixels, frames = intensity.shape
    bins_owned = NBINS // n_mod
    rows = round_up(NBINS, 16)
    chunk = min(1024, pixels)
    shape = jax.ShapeDtypeStruct
    all_bins = pixel_bin.reshape(1, n_mod * pixels)
    bins = lax.dynamic_slice_in_dim(pixel_bin, module * pixels, pixels).reshape(1, pixels)
    flops = 2 * rows * pixels * 256

    partial = call(
        functools.partial(totals_kernel, chunk=chunk), shape((rows, frames), F32), bins, intensity,
        flops=flops,
    )
    others = [swap(partial, "mod", s) for s in range(1, n_mod)]
    counts, flipped = call(
        functools.partial(prepare_kernel, chunk=chunk),
        (shape((rows, 128), F32), shape((frames, pixels), BF16)),
        all_bins, intensity, flops=flops,
    )
    pooled = call(
        functools.partial(pool_kernel, chunk=chunk), shape((TBIN, pixels), BF16),
        bins, counts, flipped, partial, *others, flops=flops,
    )
    every = gather_blocks(pooled)
    stride = round_up(bins_owned, 8)
    owner = bins // bins_owned
    placed = (owner ^ module) * stride + (bins - owner * bins_owned)
    group = min(32, every.shape[0])
    grams = [
        call(
            functools.partial(gram_kernel, chunk=chunk),
            shape((n_mod * stride, TBIN * group), F32),
            placed, pooled, every[g : g + group], flops=flops,
        ).reshape(n_mod, stride, TBIN, group)
        for g in range(0, every.shape[0], group)
    ]
    gram = grams[0] if len(grams) == 1 else jnp.concatenate(grams, axis=3)
    gram = gram.reshape(n_mod, stride, TBIN * every.shape[0])
    total = gram[0]
    for s in range(1, n_mod):
        total = total + swap(gram[s], "mod", s)
    own_counts = lax.dynamic_slice_in_dim(counts, module * bins_owned, bins_owned)[:, :1]
    result = total[:bins_owned] / jnp.maximum(own_counts, 1.0)
    return result.reshape(bins_owned, TBIN, every.shape[0])


def solution(mesh):
    in_specs = (P("mod", "blk"), P())
    out_specs = P("mod", "blk", None)
    return jax.shard_map(body, mesh=mesh, in_specs=in_specs, out_specs=out_specs, check_vma=False)
```

time: 323 us -> 37.8 us (0.12)
  local copies, waits for them, and re-layouts: 250 us -> 3.63 us
  matrix products: 29 us -> 0 us
  other arithmetic: 23.6 us -> 1.91 us
  between operations: 13.2 us -> 0.13 us
  Pallas kernels: 0 us -> 9.76 us
  waiting for transfers between devices: 0.02 us -> 9.37 us
  starting transfers between devices: 5.15 us -> 12.8 us
    gather x3 -> x1, local copies, waits for them, and re-layouts: 196 us -> 0.99 us  [gather_blocks(): return flat[order].reshape(n_blk * pooled.shape[0], pooled.shape[1])]
    dot_general x4 -> x0, matrix products: 29 us -> none  [the longest x1 10.7 us: body(): jnp.dot(onehot_wide, bin_means, precision=highest) + (1.0 - has_bin)]
    sort x4 -> x0, local copies, waits for them, and re-layouts: 27 us -> none  [first_members(): order = jnp.argsort(sort_keys, axis=1, stable=True)[:, :slot_size]]
    ppermute x0 -> x10, starting transfers between devices: none -> 12.8 us  [swap(): return lax.ppermute(value, axis, [(i, i ^ distance) for i in range(size)])]
    dot_general x1 -> x0, local copies, waits for them, and re-layouts: 11.9 us -> none  [body(): lax.dot_general(expanded, piece, (((0,), (1,)), ((), ())), preferred_elem...]
    mul x1 -> x0, local copies, waits for them, and re-layouts: 11.4 us -> none  [body(): owner_onehot[:, :, None] * pooled.T[:, None, :]]
    select_n x5 -> x1, other arithmetic: 10.6 us -> 0.01 us  [gather_blocks(): return flat[order].reshape(n_blk * pooled.shape[0], pooled.shape[1])]
    pallas_call x0 -> x4, Pallas kernels: none -> 9.76 us  [call(): pl.pallas_call(kernel, out_shape=out_shape, in_specs=[vmem] * len(args),...]
  transfers between devices with their start and end apart: 2 -> 10, of which waited for: 0 -> 7; matrix products, arithmetic and copies ran while one was open for 54% -> 1% of each run, Pallas kernels for 0% -> 14%
where the time goes in v1:
time: 37.8 us; the launch traced here: 37.6 us
  starting transfers between devices  12.8 us (34%)
  Pallas kernels  9.76 us (26%)
  waiting for transfers between devices  9.37 us (25%)
  local copies, waits for them, and re-layouts  3.63 us (10%)
  other arithmetic  1.91 us (5%)
    ppermute x10, starting transfers between devices, swap(): return lax.ppermute(value, axis, [(i, i ^ distance) for i in range(size)])  12.8 us
    pallas_call x4, Pallas kernels, call(): pl.pallas_call(kernel, out_shape=out_shape, in_specs=[vmem] * len(args),...  9.76 us
    ppermute x10, waiting for transfers between devices, swap(): return lax.ppermute(value, axis, [(i, i ^ distance) for i in range(size)])  9.37 us
    unnamed x4, local copies, waits for them, and re-layouts  1.59 us
    gather x1, local copies, waits for them, and re-layouts, gather_blocks(): return flat[order].reshape(n_blk * pooled.shape[0], pooled.shape[1])  0.99 us
    add x1, other arithmetic, body(): placed = (owner ^ module) * stride + (bins - owner * bins_owned)  0.86 us
  transfers between devices with their start and end apart: 10, of which 7 were waited for; matrix products, arithmetic and copies ran while one was open for 1% of the time, Pallas kernels for 14%

profile of v1, /device:TPU:0, one launch (start us, length us, event | category | flops | bytes accessed | tf_op | source)
XLA Modules:
  0.0 37.6 jit_solution(3075204511152736615)
XLA Ops:
  0.0 0.9 %subtract_add_fusion = (s32[8192]{0:T(1024)S(1)}, s32[8192]{0:T(1024)S(1)}) fusion(s32[]{:T(128)S(6)} %axis_index.23, s32[32768]{0:T(1024)} %param.3, s32[]{:T(128)S(6)} %select_n.22), kind=kLoop, calls=%fused_computation.4 | loop fusion | flops 106496 | bytes 98312 | tf_op jit(solution)/shard_map/add | solution.py:173
  0.9 1.6 %copy-done.1 = bf16[8192,128]{1,0:T(8,128)(2,1)S(1)} copy-done((bf16[8192,128]{1,0:T(8,128)(2,1)S(1)}, bf16[8192,128]{1,0:T(8,128)(2,1)}, u32[]{:S(2)}) %copy-start.1) | copy-done | bytes 2097176
  2.5 1.0 %shard_map.29.own_ref = f32[208,128]{1,0:T(8,128)S(1)} custom-call(s32[1,8192]{1,0:T(1,128)S(1)} %bitcast.17, bf16[8192,128]{1,0:T(8,128)(2,1)S(1)} %copy-done.1), custom_call_target="tpu_custom_call" | custom-call | flops 872415232 | bytes 2236416 | tf_op jit(solution)/shard_map/pallas_call | solution.py:114
  3.5 3.0 %collective-permute-start = (f32[208,128]{1,0:T(8,128)S(1)}, f32[208,128]{1,0:T(8,128)S(1)}, u32[]{:S(2)}, u32[]{:S(2)}) collective-permute-start(f32[208,128]{1,0:T(8,128)S(1)} %shard_map.29.own_ref), channel_id=1, source_target_pairs={{0,8},{8,0},{16,24},{24,16},{1,9},{9,1},{17,25},{25,17},{2,10},{10... | collective-permute-start | bytes 319496 | tf_op jit(solution)/shard_map/ppermute | solution.py:126
  6.5 1.5 %collective-permute-start.1 = (f32[208,128]{1,0:T(8,128)S(1)}, f32[208,128]{1,0:T(8,128)S(1)}, u32[]{:S(2)}, u32[]{:S(2)}) collective-permute-start(f32[208,128]{1,0:T(8,128)S(1)} %shard_map.29.own_ref), channel_id=1, source_target_pairs={{0,16},{8,24},{16,0},{24,8},{1,17},{9,25},{17,1},{25,9},{2,18},{10... | collective-permute-start | bytes 319496 | tf_op jit(solution)/shard_map/ppermute | solution.py:126
  8.0 5.4 %shard_map.28 = (f32[208,128]{1,0:T(8,128)S(1)}, bf16[128,8192]{1,0:T(8,128)(2,1)S(1)}) custom-call(s32[1,32768]{1,0:T(1,128)S(1)} %bitcast.19, bf16[8192,128]{1,0:T(8,128)(2,1)S(1)} %copy-done.1), custom_call_target="tpu_custom_call" | custom-call | flops 872415232 | bytes 4431872 | tf_op jit(solution)/shard_map/pallas_call | solution.py:114
  13.6 1.9 %shard_map.30.own_ref = bf16[4,8192]{1,0:T(4,128)(2,1)S(1)} custom-call(s32[1,8192]{1,0:T(1,128)S(1)} %bitcast.18, f32[208,128]{1,0:T(8,128)S(1)} %get-tuple-element.7.counts_ref, bf16[128,8192]{1,0:T(8,128)(2,1)S(1)} %get-tuple-element.8.flipped_ref, f32[208,128]{1,0:T(8,128)S(1)} %shard_map.29.own_ref, f32[208,128]{1,0:T(8,128)S(1)} %collective-permute-done.rest_0_, ...), custom_call_target="tpu_custom_call" | custom-call | flops 872415232 | bytes 2727936 | tf_op jit(solution)/shard_map/pallas_call | solution.py:114
  15.5 4.0 %collective-permute-start.5 = (bf16[4,8192]{1,0:T(4,128)(2,1)S(1)}, bf16[4,8192]{1,0:T(4,128)(2,1)S(1)}, u32[]{:S(2)}, u32[]{:S(2)}) collective-permute-start(bf16[4,8192]{1,0:T(4,128)(2,1)S(1)} %shard_map.30.own_ref), channel_id=1, source_target_pairs={{0,6},{1,7},{2,4},{3,5},{4,2},{5,3},{6,0},{7,1},{8,14},{9,15},{10,... | collective-permute-start | bytes 196616 | tf_op jit(solution)/shard_map/ppermute | solution.py:126
  19.5 0.6 %collective-permute-start.3 = (bf16[4,8192]{1,0:T(4,128)(2,1)S(1)}, bf16[4,8192]{1,0:T(4,128)(2,1)S(1)}, u32[]{:S(2)}, u32[]{:S(2)}) collective-permute-start(bf16[4,8192]{1,0:T(4,128)(2,1)S(1)} %shard_map.30.own_ref), channel_id=1, source_target_pairs={{0,2},{1,3},{2,0},{3,1},{4,6},{5,7},{6,4},{7,5},{8,10},{9,11},{10,... | collective-permute-start | bytes 196616 | tf_op jit(solution)/shard_map/ppermute | solution.py:126
  20.2 2.1 %collective-permute-done.5 = bf16[4,8192]{1,0:T(4,128)(2,1)S(1)} collective-permute-done((bf16[4,8192]{1,0:T(4,128)(2,1)S(1)}, bf16[4,8192]{1,0:T(4,128)(2,1)S(1)}, u32[]{:S(2)}, u32[]{:S(2)}) %collective-permute-start.5) | collective-permute-done | bytes 65568 | tf_op jit(solution)/shard_map/ppermute | solution.py:126
  22.2 2.6 %collective-permute-done.4 = bf16[4,8192]{1,0:T(4,128)(2,1)S(1)} collective-permute-done((bf16[4,8192]{1,0:T(4,128)(2,1)S(1)}, bf16[4,8192]{1,0:T(4,128)(2,1)S(1)}, u32[]{:S(2)}, u32[]{:S(2)}) %collective-permute-start.4) | collective-permute-done | bytes 65568 | tf_op jit(solution)/shard_map/ppermute | solution.py:126
  24.9 0.2 pad_maximum_fusion.1
  25.2 0.2 fusion.5
  25.4 1.3 %collective-permute-done.6 = bf16[4,4,8192]{2,1,0:T(4,128)(2,1)S(1)} collective-permute-done((bf16[4,4,8192]{2,1,0:T(4,128)(2,1)S(1)}, bf16[4,4,8192]{2,1,0:T(4,128)(2,1)S(1)}, u32[]{:S(2)}, u32[]{:S(2)}) %collective-permute-start.6) | collective-permute-done | bytes 262176 | tf_op jit(solution)/shard_map/ppermute | solution.py:126
  26.7 0.4 pad_maximum_fusion
  27.3 1.0 %gather_fusion = bf16[8,4,8192]{2,1,0:T(4,128)(2,1)S(1)} fusion(bf16[8,4,8192]{2,1,0:T(4,128)(2,1)S(1)} %bitcast.20, s32[1024]{0:T(1024)S(1)} %pad_clamp_fusion), kind=kCustom, calls=%fused_computation | custom fusion | bytes 1048608 | tf_op jit(solution)/shard_map/gather | solution.py:140
  28.4 1.5 %shard_map.31 = f32[224,128]{1,0:T(8,128)S(1)} custom-call(s32[1,8192]{1,0:T(1,128)S(1)} %bitcast.16, bf16[4,8192]{1,0:T(4,128)(2,1)S(1)} %shard_map.30.own_ref, bf16[32,8192]{1,0:T(8,128)(2,1)S(1)} %reshape.55.all_ref), custom_call_target="tpu_custom_call" | custom-call | flops 872415232 | bytes 737280 | tf_op jit(solution)/shard_map/pallas_call | solution.py:114
  29.9 2.5 %collective-permute-start.9 = (f32[56,128]{1,0:T(8,128)S(1)}, f32[56,128]{1,0:T(8,128)S(1)}, u32[]{:S(2)}, u32[]{:S(2)}) collective-permute-start(f32[56,128]{1,0:T(8,128)S(1)} %get-tuple-element.12), channel_id=1, source_target_pairs={{0,24},{8,16},{16,8},{24,0},{1,25},{9,17},{17,9},{25,1},{2,26},{10... | collective-permute-start | bytes 86024 | tf_op jit(solution)/shard_map/ppermute | solution.py:126
  32.4 0.5 %collective-permute-start.8 = (f32[56,128]{1,0:T(8,128)S(1)}, f32[56,128]{1,0:T(8,128)S(1)}, u32[]{:S(2)}, u32[]{:S(2)}) collective-permute-start(f32[56,128]{1,0:T(8,128)S(1)} %get-tuple-element.13), channel_id=1, source_target_pairs={{0,16},{8,24},{16,0},{24,8},{1,17},{9,25},{17,1},{25,9},{2,18},{10... | collective-permute-start | bytes 86024 | tf_op jit(solution)/shard_map/ppermute | solution.py:126
  32.9 0.5 %collective-permute-start.7 = (f32[56,128]{1,0:T(8,128)S(1)}, f32[56,128]{1,0:T(8,128)S(1)}, u32[]{:S(2)}, u32[]{:S(2)}) collective-permute-start(f32[56,128]{1,0:T(8,128)S(1)} %get-tuple-element.14), channel_id=1, source_target_pairs={{0,8},{8,0},{16,24},{24,16},{1,9},{9,1},{17,25},{25,17},{2,10},{10... | collective-permute-start | bytes 86024 | tf_op jit(solution)/shard_map/ppermute | solution.py:126
  33.6 1.2 %collective-permute-done.9 = f32[56,128]{1,0:T(8,128)S(1)} collective-permute-done((f32[56,128]{1,0:T(8,128)S(1)}, f32[56,128]{1,0:T(8,128)S(1)}, u32[]{:S(2)}, u32[]{:S(2)}) %collective-permute-start.9) | collective-permute-done | bytes 28704 | tf_op jit(solution)/shard_map/ppermute | solution.py:126
  34.7 1.6 %collective-permute-done.8 = f32[56,128]{1,0:T(8,128)S(1)} collective-permute-done((f32[56,128]{1,0:T(8,128)S(1)}, f32[56,128]{1,0:T(8,128)S(1)}, u32[]{:S(2)}, u32[]{:S(2)}) %collective-permute-start.8) | collective-permute-done | bytes 28704 | tf_op jit(solution)/shard_map/ppermute | solution.py:126
  36.3 0.5 %collective-permute-done.7 = f32[56,128]{1,0:T(8,128)S(1)} collective-permute-done((f32[56,128]{1,0:T(8,128)S(1)}, f32[56,128]{1,0:T(8,128)S(1)}, u32[]{:S(2)}, u32[]{:S(2)}) %collective-permute-start.7) | collective-permute-done | bytes 28704 | tf_op jit(solution)/shard_map/ppermute | solution.py:126
  36.9 0.7 %copy.5 = f32[50,128]{0,1:T(8,128)} copy(f32[50,128]{1,0:T(8,128)S(1)} %fusion.2) | data formatting | bytes 51200 | tf_op jit(solution)/shard_map/div | solution.py:189
  (17 shorter events, 0.8 us)
Async XLA Ops:
  0.0 8.0 %copy-start = (s32[32768]{0:T(1024)S(1)}, s32[32768]{0:T(1024)}, u32[]{:S(2)}) copy-start(s32[32768]{0:T(1024)} %param.3) | copy-start | bytes 393220
  0.9 1.6 %copy-start.1 = (bf16[8192,128]{1,0:T(8,128)(2,1)S(1)}, bf16[8192,128]{1,0:T(8,128)(2,1)}, u32[]{:S(2)}) copy-start(bf16[8192,128]{1,0:T(8,128)(2,1)} %intensity_ref.3) | copy-start | bytes 6291460
  3.5 10.0 %collective-permute-start = (f32[208,128]{1,0:T(8,128)S(1)}, f32[208,128]{1,0:T(8,128)S(1)}, u32[]{:S(2)}, u32[]{:S(2)}) collective-permute-start(f32[208,128]{1,0:T(8,128)S(1)} %shard_map.29.own_ref), channel_id=1, source_target_pairs={{0,8},{8,0},{16,24},{24,16},{1,9},{9,1},{17,25},{25,17},{2,10},{10... | collective-permute-start | bytes 319496 | tf_op jit(solution)/shard_map/ppermute | solution.py:126
  6.5 7.0 %collective-permute-start.1 = (f32[208,128]{1,0:T(8,128)S(1)}, f32[208,128]{1,0:T(8,128)S(1)}, u32[]{:S(2)}, u32[]{:S(2)}) collective-permute-start(f32[208,128]{1,0:T(8,128)S(1)} %shard_map.29.own_ref), channel_id=1, source_target_pairs={{0,16},{8,24},{16,0},{24,8},{1,17},{9,25},{17,1},{25,9},{2,18},{10... | collective-permute-start | bytes 319496 | tf_op jit(solution)/shard_map/ppermute | solution.py:126
  8.0 5.6 %collective-permute-start.2 = (f32[208,128]{1,0:T(8,128)S(1)}, f32[208,128]{1,0:T(8,128)S(1)}, u32[]{:S(2)}, u32[]{:S(2)}) collective-permute-start(f32[208,128]{1,0:T(8,128)S(1)} %shard_map.29.own_ref), channel_id=1, source_target_pairs={{0,24},{8,16},{16,8},{24,0},{1,25},{9,17},{17,9},{25,1},{2,26},{10... | collective-permute-start | bytes 319496 | tf_op jit(solution)/shard_map/ppermute | solution.py:126
  15.5 6.7 %collective-permute-start.5 = (bf16[4,8192]{1,0:T(4,128)(2,1)S(1)}, bf16[4,8192]{1,0:T(4,128)(2,1)S(1)}, u32[]{:S(2)}, u32[]{:S(2)}) collective-permute-start(bf16[4,8192]{1,0:T(4,128)(2,1)S(1)} %shard_map.30.own_ref), channel_id=1, source_target_pairs={{0,6},{1,7},{2,4},{3,5},{4,2},{5,3},{6,0},{7,1},{8,14},{9,15},{10,... | collective-permute-start | bytes 196616 | tf_op jit(solution)/shard_map/ppermute | solution.py:126
  19.5 5.4 %collective-permute-start.4 = (bf16[4,8192]{1,0:T(4,128)(2,1)S(1)}, bf16[4,8192]{1,0:T(4,128)(2,1)S(1)}, u32[]{:S(2)}, u32[]{:S(2)}) collective-permute-start(bf16[4,8192]{1,0:T(4,128)(2,1)S(1)} %shard_map.30.own_ref), channel_id=1, source_target_pairs={{0,4},{1,5},{2,6},{3,7},{4,0},{5,1},{6,2},{7,3},{8,12},{9,13},{10,... | collective-permute-start | bytes 196616 | tf_op jit(solution)/shard_map/ppermute | solution.py:126
  19.5 5.4 %collective-permute-start.3 = (bf16[4,8192]{1,0:T(4,128)(2,1)S(1)}, bf16[4,8192]{1,0:T(4,128)(2,1)S(1)}, u32[]{:S(2)}, u32[]{:S(2)}) collective-permute-start(bf16[4,8192]{1,0:T(4,128)(2,1)S(1)} %shard_map.30.own_ref), channel_id=1, source_target_pairs={{0,2},{1,3},{2,0},{3,1},{4,6},{5,7},{6,4},{7,5},{8,10},{9,11},{10,... | collective-permute-start | bytes 196616 | tf_op jit(solution)/shard_map/ppermute | solution.py:126
  25.1 1.6 %collective-permute-start.6 = (bf16[4,4,8192]{2,1,0:T(4,128)(2,1)S(1)}, bf16[4,4,8192]{2,1,0:T(4,128)(2,1)S(1)}, u32[]{:S(2)}, u32[]{:S(2)}) collective-permute-start(bf16[4,4,8192]{2,1,0:T(4,128)(2,1)S(1)} %pad_maximum_fusion.1), channel_id=1, source_target_pairs={{0,1},{1,0},{2,3},{3,2},{4,5},{5,4},{6,7},{7,6},{8,9},{9,8},{10,11... | collective-permute-start | bytes 786440 | tf_op jit(solution)/shard_map/ppermute | solution.py:126
  29.9 4.8 %collective-permute-start.9 = (f32[56,128]{1,0:T(8,128)S(1)}, f32[56,128]{1,0:T(8,128)S(1)}, u32[]{:S(2)}, u32[]{:S(2)}) collective-permute-start(f32[56,128]{1,0:T(8,128)S(1)} %get-tuple-element.12), channel_id=1, source_target_pairs={{0,24},{8,16},{16,8},{24,0},{1,25},{9,17},{17,9},{25,1},{2,26},{10... | collective-permute-start | bytes 86024 | tf_op jit(solution)/shard_map/ppermute | solution.py:126
  32.4 3.9 %collective-permute-start.8 = (f32[56,128]{1,0:T(8,128)S(1)}, f32[56,128]{1,0:T(8,128)S(1)}, u32[]{:S(2)}, u32[]{:S(2)}) collective-permute-start(f32[56,128]{1,0:T(8,128)S(1)} %get-tuple-element.13), channel_id=1, source_target_pairs={{0,16},{8,24},{16,0},{24,8},{1,17},{9,25},{17,1},{25,9},{2,18},{10... | collective-permute-start | bytes 86024 | tf_op jit(solution)/shard_map/ppermute | solution.py:126
  32.9 3.9 %collective-permute-start.7 = (f32[56,128]{1,0:T(8,128)S(1)}, f32[56,128]{1,0:T(8,128)S(1)}, u32[]{:S(2)}, u32[]{:S(2)}) collective-permute-start(f32[56,128]{1,0:T(8,128)S(1)} %get-tuple-element.14), channel_id=1, source_target_pairs={{0,8},{8,0},{16,24},{24,16},{1,9},{9,1},{17,25},{25,17},{2,10},{10... | collective-permute-start | bytes 86024 | tf_op jit(solution)/shard_map/ppermute | solution.py:126

commit v2 on v1

v2 whole, which is shorter than its diff:
```python
import functools

import jax
import jax.numpy as jnp
from jax import lax
from jax.experimental import pallas as pl
from jax.experimental.pallas import tpu as pltpu
from jax.sharding import PartitionSpec as P

NBINS = 200
TBIN = 4
GROUP = 8
F32 = jnp.float32
BF16 = jnp.bfloat16
NT = (((1,), (1,)), ((), ()))
TN = (((0,), (0,)), ((), ()))
VMEM = pl.BlockSpec(memory_space=pltpu.VMEM)
HBM = pl.BlockSpec(memory_space=pltpu.HBM)


def round_up(value, multiple):
    return (value + multiple - 1) // multiple * multiple


def onehot_rows(index_row, rows):
    row_ids = lax.broadcasted_iota(jnp.int32, (rows, index_row.shape[1]), 0)
    return jnp.where(row_ids == index_row, 1.0, 0.0).astype(BF16)


def split_hi_lo(value):
    hi = value.astype(BF16)
    lo = (value - hi.astype(F32)).astype(BF16)
    return hi, lo


def totals_kernel(
    bins_hbm, intensity_hbm, out_ref, onehot_ref, kept_ref, bins_ref, bins_sem, intensity_sem, *, chunk
):
    rows, pixels = onehot_ref.shape
    bins_copy = pltpu.make_async_copy(bins_hbm, bins_ref, bins_sem)
    bins_copy.start()
    intensity_copy = pltpu.make_async_copy(intensity_hbm, kept_ref, intensity_sem)
    intensity_copy.start()
    bins_copy.wait()
    module = lax.axis_index("mod")
    for start in range(0, pixels, chunk):
        part = slice(start, start + chunk)
        onehot_ref[:, part] = onehot_rows(bins_ref[module, :, part], rows)
    intensity_copy.wait()
    total = jnp.dot(onehot_ref[...], kept_ref[...], preferred_element_type=F32)
    out_ref[...] = total[: out_ref.shape[0], :]


def prepare_kernel(
    bins_ref, intensity_ref, onehot_ref, counts_ref, flipped_ref, by_pixel_ref, *, chunk
):
    rows, lanes = counts_ref.shape
    frames = intensity_ref.shape[1]
    digits = 16
    hist = jnp.zeros((digits, digits), F32)
    starts = range(0, bins_ref.shape[2], chunk)
    for module, start in [(m, start) for m in range(bins_ref.shape[0]) for start in starts]:
        piece = bins_ref[module, :, start : start + chunk]
        high = onehot_rows(piece // digits, digits)
        low = onehot_rows(piece % digits, digits)
        hist += lax.dot_general(high, low, NT, preferred_element_type=F32)
    row_ids = lax.broadcasted_iota(jnp.int32, (rows, digits), 0)
    digit_ids = lax.broadcasted_iota(jnp.int32, (rows, digits), 1)
    spread = jnp.where(row_ids // digits == digit_ids, 1.0, 0.0).astype(F32)
    by_low = jnp.dot(spread, hist, precision=lax.Precision.HIGHEST, preferred_element_type=F32)
    counts = jnp.sum(jnp.where(row_ids % digits == digit_ids, by_low, 0.0), axis=1, keepdims=True)
    counts_ref[...] = jnp.broadcast_to(counts, (rows, lanes))
    eye = (
        lax.broadcasted_iota(jnp.int32, (frames, frames), 0)
        == lax.broadcasted_iota(jnp.int32, (frames, frames), 1)
    )
    eye = jnp.where(eye, 1.0, 0.0).astype(BF16)
    for start in range(0, intensity_ref.shape[0], chunk):
        block = intensity_ref[start : start + chunk, :]
        flipped_ref[:, start : start + chunk] = lax.dot_general(
            eye, block, NT, preferred_element_type=F32
        )
        by_pixel_ref[start : start + chunk, :] = onehot_ref[:, start : start + chunk].T


def pool_kernel(counts_ref, onehot_ref, flipped_ref, own_ref, *rest, chunk):
    *other_refs, out_ref = rest
    rows = onehot_ref.shape[0]
    frames, pixels = flipped_ref.shape
    totals = own_ref[...]
    for other in other_refs:
        totals += other[...]
    totals = jnp.concatenate([totals, jnp.ones((rows - totals.shape[0], frames), F32)], axis=0)
    pool = frames // out_ref.shape[0]
    weights = counts_ref[...] / (totals * float(pool))
    hi, lo = split_hi_lo(weights)
    both = jnp.concatenate([hi, lo], axis=1)
    for start in range(0, pixels, chunk):
        part = slice(start, start + chunk)
        spread = lax.dot_general(both, onehot_ref[:, part], TN, preferred_element_type=F32)
        ratios = flipped_ref[:, part] * (spread[:frames, :] + spread[frames:, :])
        pooled = [
            jnp.sum(ratios[i * pool : (i + 1) * pool, :], axis=0, keepdims=True)
            for i in range(out_ref.shape[0])
        ]
        out_ref[:, part] = jnp.concatenate(pooled, axis=0).astype(BF16)


def gram_part(by_pixel_ref, own_ref, piece_refs, chunk):
    width = TBIN * TBIN * len(piece_refs)
    acc = jnp.zeros((2 * width, by_pixel_ref.shape[1]), F32)
    for start in range(0, by_pixel_ref.shape[0], chunk):
        part = slice(start, start + chunk)
        own = own_ref[:, part].astype(F32)
        every = jnp.concatenate([ref[:, part].astype(F32) for ref in piece_refs], axis=0)
        his, los = [], []
        for i in range(TBIN):
            hi, lo = split_hi_lo(own[i : i + 1, :] * every)
            his.append(hi)
            los.append(lo)
        products = jnp.concatenate(his + los, axis=0)
        acc += jnp.dot(products, by_pixel_ref[part, :], preferred_element_type=F32)
    return acc[:width, :] + acc[width:, :]


def gram_first_kernel(by_pixel_ref, own_ref, *rest, chunk):
    *piece_refs, out_ref = rest
    out_ref[...] = gram_part(by_pixel_ref, own_ref, piece_refs, chunk)


def gram_second_kernel(by_pixel_ref, own_ref, first_ref, *rest, n_mod, chunk):
    piece_refs, out_refs, whole_ref = rest[: -n_mod - 1], rest[-n_mod - 1 : -1], rest[-1]
    second = gram_part(by_pixel_ref, own_ref, piece_refs, chunk)
    whole_ref[...] = jnp.concatenate([first_ref[...], second], axis=0).T
    module = lax.axis_index("mod")
    owned = out_refs[0].shape[0]
    for s in range(n_mod):
        out_refs[s][...] = whole_ref[pl.ds((module ^ s) * owned, owned), :]


def final_kernel(counts_ref, *rest, distances):
    *in_refs, out_ref = rest
    owned, lanes = in_refs[0].shape
    total = in_refs[0][...]
    for ref in in_refs[1:]:
        total += ref[...]
    counts = counts_ref[pl.ds(lax.axis_index("mod") * owned, owned), :]
    total = total / jnp.maximum(counts, 1.0)
    out_row = lax.broadcasted_iota(jnp.int32, (lanes, lanes), 0)
    lane = lax.broadcasted_iota(jnp.int32, (lanes, lanes), 1)
    pieces = len(distances[0])
    per_half = TBIN * TBIN * pieces
    half, i = lane // per_half, lane % per_half // (TBIN * pieces)
    piece, row = lane % (TBIN * pieces) // TBIN, lane % TBIN
    block = jnp.zeros_like(lane)
    for h in range(2):
        for n in range(pieces):
            block = jnp.where((half == h) & (piece == n), distances[h][n], block)
    if pieces * 2 == lax.axis_size("blk"):
        block ^= lax.axis_index("blk")
    place = jnp.where(out_row == i * (TBIN * GROUP) + block * TBIN + row, 1.0, 0.0).astype(F32)
    out_ref[...] = lax.dot_general(
        place, total, NT, precision=lax.Precision.HIGHEST, preferred_element_type=F32
    )


def call(kernel, outs, *args, flops, in_specs=None, out_specs=None, scratch=()):
    moved = sum(a.size * a.dtype.itemsize for a in args)
    moved += sum(s.size * s.dtype.itemsize for s in outs)
    result = pl.pallas_call(
        kernel,
        out_shape=tuple(outs),
        in_specs=in_specs or [VMEM] * len(args),
        out_specs=out_specs or (VMEM,) * len(outs),
        scratch_shapes=list(scratch),
        compiler_params=pltpu.CompilerParams(vmem_limit_bytes=32 << 20),
        cost_estimate=pl.CostEstimate(flops=flops, bytes_accessed=moved, transcendentals=0),
    )(*args)
    return result if len(outs) > 1 else result[0]


def swap(value, axis, distance):
    size = lax.axis_size(axis)
    return lax.ppermute(value, axis, [(i, i ^ distance) for i in range(size)])


def body(intensity, pixel_bin):
    n_mod = lax.axis_size("mod")
    pixels, frames = intensity.shape
    bins_owned = NBINS // n_mod
    rows = round_up(NBINS, 16)
    chunk = min(1024, pixels)
    shape = jax.ShapeDtypeStruct
    flops = 2 * rows * pixels * 256

    mod_order = (1, 3, 2) if n_mod == 4 else tuple(range(1, n_mod))
    partial, onehot, kept, bins = call(
        functools.partial(totals_kernel, chunk=chunk),
        [
            shape((NBINS, frames), F32),
            shape((rows, pixels), BF16),
            shape((pixels, frames), BF16),
            shape((n_mod, 1, pixels), jnp.int32),
        ],
        pltpu.with_memory_space_constraint(pixel_bin.reshape(n_mod, 1, pixels), pltpu.HBM),
        pltpu.with_memory_space_constraint(intensity, pltpu.HBM),
        flops=flops, in_specs=[HBM, HBM],
        scratch=[pltpu.SemaphoreType.DMA, pltpu.SemaphoreType.DMA],
    )
    others = [swap(partial, "mod", s) for s in mod_order]
    counts, flipped, by_pixel = call(
        functools.partial(prepare_kernel, chunk=chunk),
        [shape((rows, 128), F32), shape((frames, pixels), F32), shape((pixels, rows), BF16)],
        bins, kept, onehot, flops=flops,
    )
    pooled = call(
        functools.partial(pool_kernel, chunk=chunk), [shape((TBIN, pixels), BF16)],
        counts, onehot, flipped, partial, *others, flops=flops,
    )
    width = TBIN * TBIN * GROUP
    if lax.axis_size("blk") == GROUP:
        far = [swap(pooled, "blk", s) for s in (2, 6, 4)]
        near = swap(pooled, "blk", 1)
        passed = [swap(piece, "blk", 1) for piece in far]
        groups = [([pooled, *far], [near, *passed])]
        distances = ((0, 2, 6, 4), (1, 3, 7, 5))
    else:
        every = lax.all_gather(pooled, "blk", axis=0)
        blocks = [every[b] for b in range(every.shape[0])]
        half = GROUP // 2
        groups = [
            (blocks[g : g + half], blocks[g + half : g + GROUP]) for g in range(0, len(blocks), GROUP)
        ]
        distances = (tuple(range(half)), tuple(range(half, GROUP)))
    results = []
    for first_pieces, second_pieces in groups:
        first = call(
            functools.partial(gram_first_kernel, chunk=2 * chunk), [shape((width // 2, rows), F32)],
            by_pixel, pooled, *first_pieces, flops=flops,
        )
        blocks = call(
            functools.partial(gram_second_kernel, n_mod=n_mod, chunk=2 * chunk),
            [shape((bins_owned, width), F32)] * n_mod,
            by_pixel, pooled, first, *second_pieces, flops=flops,
            scratch=[pltpu.VMEM((rows, width), F32)],
        )
        arrived = [swap(blocks[s], "mod", s) for s in mod_order]
        columns = call(
            functools.partial(final_kernel, distances=distances),
            [shape((width, bins_owned), F32)], counts, blocks[0], *arrived, flops=flops // 64,
        )
        results.append(columns.reshape(TBIN, TBIN * GROUP, bins_owned))
    result = results[0] if len(results) == 1 else jnp.concatenate(results, axis=1)
    return jnp.transpose(result, (2, 0, 1))


def solution(mesh):
    in_specs = (P("mod", "blk"), P())
    out_specs = P("mod", "blk", None)
    return jax.shard_map(body, mesh=mesh, in_specs=in_specs, out_specs=out_specs, check_vma=False)
```

time: 37.8 us -> 34.2 us (0.905)
  local copies, waits for them, and re-layouts: 3.63 us -> 0 us
  waiting for transfers between devices: 9.37 us -> 12.5 us
  other arithmetic: 1.91 us -> 0 us
  Pallas kernels: 9.76 us -> 8.78 us
    ppermute x10 -> x13, waiting for transfers between devices: 9.37 us -> 12.5 us  [swap(): return lax.ppermute(value, axis, [(i, i ^ distance) for i in range(size)])]
    unnamed x4 -> x0, local copies, waits for them, and re-layouts: 1.59 us -> none
    gather x1 -> x0, local copies, waits for them, and re-layouts: 0.99 us -> none  [gather_blocks(): return flat[order].reshape(n_blk * pooled.shape[0], pooled.shape[1])]
    pallas_call x4 -> x6, Pallas kernels: 9.76 us -> 8.78 us  [call(): pl.pallas_call(kernel, out_shape=tuple(outs), in_specs=in_specs or [VMEM]...]
    add x1 -> x0, other arithmetic: 0.86 us -> none  [body(): placed = (owner ^ module) * stride + (bins - owner * bins_owned)]
    another operation x3 -> x0, other arithmetic: 0.84 us -> none  [the longest x2 0.61 us: gather_blocks(): pairs = jnp.stack([mine, sibling], axis=1)]
    div x1 -> x0, local copies, waits for them, and re-layouts: 0.73 us -> none  [body(): result = total[:bins_owned] / jnp.maximum(own_counts, 1.0)]
    ppermute x10 -> x13, starting transfers between devices: 12.8 us -> 12.7 us  [swap(): return lax.ppermute(value, axis, [(i, i ^ distance) for i in range(size)])]
  transfers between devices with their start and end apart: 10 -> 13, of which waited for: 7 -> 8; matrix products, arithmetic and copies ran while one was open for 1% -> 0% of each run, Pallas kernels for 14% -> 9%
where the time goes in v2:
time: 34.2 us; the launch traced here: 34.1 us
  starting transfers between devices  12.7 us (37%)
  waiting for transfers between devices  12.5 us (37%)
  Pallas kernels  8.78 us (26%)
    ppermute x13, starting transfers between devices, swap(): return lax.ppermute(value, axis, [(i, i ^ distance) for i in range(size)])  12.7 us
    ppermute x13, waiting for transfers between devices, swap(): return lax.ppermute(value, axis, [(i, i ^ distance) for i in range(size)])  12.5 us
    pallas_call x6, Pallas kernels, call(): pl.pallas_call(kernel, out_shape=tuple(outs), in_specs=in_specs or [VMEM]...  8.78 us
  transfers between devices with their start and end apart: 13, of which 8 were waited for; matrix products, arithmetic and copies ran while one was open for 0% of the time, Pallas kernels for 9%

profile of v2, /device:TPU:0, one launch (start us, length us, event | category | flops | bytes accessed | tf_op | source)
XLA Modules:
  0.0 34.1 jit_solution(4486248588960241448)
XLA Ops:
  0.0 2.7 %shard_map.28 = (f32[200,128]{1,0:T(8,128)S(1)}, bf16[208,8192]{1,0:T(8,128)(2,1)S(1)}, bf16[8192,128]{1,0:T(8,128)(2,1)S(1)}, s32[4,1,8192]{2,1,0:T(1,128)S(1)}) custom-call(s32[4,1,8192]{2,1,0:T(1,128)} %bitcast.4, bf16[8192,128]{1,0:T(8,128)(2,1)} %intensity_hbm.1), custom_call_target="tpu_custom_call" | custom-call | flops 872415232 | bytes 7966720 | tf_op jit(solution)/shard_map/pallas_call | solution.py:170
  2.7 3.0 %collective-permute-start = (f32[200,128]{1,0:T(8,128)S(1)}, f32[200,128]{1,0:T(8,128)S(1)}, u32[]{:S(2)}, u32[]{:S(2)}) collective-permute-start(f32[200,128]{1,0:T(8,128)S(1)} %get-tuple-element.22.own_ref), channel_id=1, source_target_pairs={{0,8},{8,0},{16,24},{24,16},{1,9},{9,1},{17,25},{25,17},{2,10},{10... | collective-permute-start | bytes 307208 | tf_op jit(solution)/shard_map/ppermute | solution.py:184
  5.7 1.5 %collective-permute-start.1 = (f32[200,128]{1,0:T(8,128)S(1)}, f32[200,128]{1,0:T(8,128)S(1)}, u32[]{:S(2)}, u32[]{:S(2)}) collective-permute-start(f32[200,128]{1,0:T(8,128)S(1)} %get-tuple-element.22.own_ref), channel_id=1, source_target_pairs={{0,24},{8,16},{16,8},{24,0},{1,25},{9,17},{17,9},{25,1},{2,26},{10... | collective-permute-start | bytes 307208 | tf_op jit(solution)/shard_map/ppermute | solution.py:184
  7.2 0.0 collective-permute-start.2
  7.3 2.1 %shard_map.29 = (f32[208,128]{1,0:T(8,128)S(1)}, f32[128,8192]{1,0:T(8,128)S(1)}, bf16[8192,208]{1,0:T(8,128)(2,1)S(1)}) custom-call(s32[4,1,8192]{2,1,0:T(1,128)S(1)} %get-tuple-element.16.bins_ref, bf16[8192,128]{1,0:T(8,128)(2,1)S(1)} %get-tuple-element.17.intensity_ref, bf16[208,8192]{1,0:T(8,128)(2,1)S(1)} %get-tuple-element.18.onehot_ref), custom_call_target="tpu_custom_call" | custom-call | flops 872415232 | bytes 13344768 | tf_op jit(solution)/shard_map/pallas_call | solution.py:170
  9.4 2.8 %collective-permute-done.1.rest_1_ = f32[200,128]{1,0:T(8,128)S(1)} collective-permute-done((f32[200,128]{1,0:T(8,128)S(1)}, f32[200,128]{1,0:T(8,128)S(1)}, u32[]{:S(2)}, u32[]{:S(2)}) %collective-permute-start.1) | collective-permute-done | bytes 102432 | tf_op jit(solution)/shard_map/ppermute | solution.py:184
  12.2 1.2 %collective-permute-done.2.rest_2_ = f32[200,128]{1,0:T(8,128)S(1)} collective-permute-done((f32[200,128]{1,0:T(8,128)S(1)}, f32[200,128]{1,0:T(8,128)S(1)}, u32[]{:S(2)}, u32[]{:S(2)}) %collective-permute-start.2) | collective-permute-done | bytes 102432 | tf_op jit(solution)/shard_map/ppermute | solution.py:184
  13.3 1.3 %shard_map.30.own_ref.rest_0_ = bf16[4,8192]{1,0:T(4,128)(2,1)S(1)} custom-call(f32[208,128]{1,0:T(8,128)S(1)} %get-tuple-element.19.counts_ref, bf16[208,8192]{1,0:T(8,128)(2,1)S(1)} %get-tuple-element.18.onehot_ref, f32[128,8192]{1,0:T(8,128)S(1)} %get-tuple-element.21.flipped_ref, f32[200,128]{1,0:T(8,128)S(1)} %get-tuple-element.22.own_ref, ...), custom_call_target="tpu_custom_call" | custom-call | flops 872415232 | bytes 8183808 | tf_op jit(solution)/shard_map/pallas_call | solution.py:170
  14.7 1.6 %collective-permute-start.3 = (bf16[4,8192]{1,0:T(4,128)(2,1)S(1)}, bf16[4,8192]{1,0:T(4,128)(2,1)S(1)}, u32[]{:S(2)}, u32[]{:S(2)}) collective-permute-start(bf16[4,8192]{1,0:T(4,128)(2,1)S(1)} %shard_map.30.own_ref.rest_0_), channel_id=1, source_target_pairs={{0,2},{1,3},{2,0},{3,1},{4,6},{5,7},{6,4},{7,5},{8,10},{9,11},{10,... | collective-permute-start | bytes 196616 | tf_op jit(solution)/shard_map/ppermute | solution.py:184
  16.3 2.5 %collective-permute-start.4 = (bf16[4,8192]{1,0:T(4,128)(2,1)S(1)}, bf16[4,8192]{1,0:T(4,128)(2,1)S(1)}, u32[]{:S(2)}, u32[]{:S(2)}) collective-permute-start(bf16[4,8192]{1,0:T(4,128)(2,1)S(1)} %shard_map.30.own_ref.rest_0_), channel_id=1, source_target_pairs={{0,6},{1,7},{2,4},{3,5},{4,2},{5,3},{6,0},{7,1},{8,14},{9,15},{10,... | collective-permute-start | bytes 196616 | tf_op jit(solution)/shard_map/ppermute | solution.py:184
  18.8 0.1 collective-permute-start.5
  18.9 0.1 collective-permute-done.3.rest_1_
  19.0 0.4 %collective-permute-start.7 = (bf16[4,8192]{1,0:T(4,128)(2,1)S(1)}, bf16[4,8192]{1,0:T(4,128)(2,1)S(1)}, u32[]{:S(2)}, u32[]{:S(2)}) collective-permute-start(bf16[4,8192]{1,0:T(4,128)(2,1)S(1)} %collective-permute-done.3.rest_1_), channel_id=1, source_target_pairs={{0,1},{1,0},{2,3},{3,2},{4,5},{5,4},{6,7},{7,6},{8,9},{9,8},{10,11... | collective-permute-start | bytes 196616 | tf_op jit(solution)/shard_map/ppermute | solution.py:184
  19.4 3.1 %collective-permute-done.4.rest_2_ = bf16[4,8192]{1,0:T(4,128)(2,1)S(1)} collective-permute-done((bf16[4,8192]{1,0:T(4,128)(2,1)S(1)}, bf16[4,8192]{1,0:T(4,128)(2,1)S(1)}, u32[]{:S(2)}, u32[]{:S(2)}) %collective-permute-start.4) | collective-permute-done | bytes 65568 | tf_op jit(solution)/shard_map/ppermute | solution.py:184
  22.5 2.1 %collective-permute-done.5.rest_3_ = bf16[4,8192]{1,0:T(4,128)(2,1)S(1)} collective-permute-done((bf16[4,8192]{1,0:T(4,128)(2,1)S(1)}, bf16[4,8192]{1,0:T(4,128)(2,1)S(1)}, u32[]{:S(2)}, u32[]{:S(2)}) %collective-permute-start.5) | collective-permute-done | bytes 65568 | tf_op jit(solution)/shard_map/ppermute | solution.py:184
  24.7 0.9 %shard_map.31.first_ref = f32[64,208]{1,0:T(8,128)S(1)} custom-call(bf16[8192,208]{1,0:T(8,128)(2,1)S(1)} %get-tuple-element.20.by_pixel_ref, bf16[4,8192]{1,0:T(4,128)(2,1)S(1)} %shard_map.30.own_ref.rest_0_, bf16[4,8192]{1,0:T(4,128)(2,1)S(1)} %shard_map.30.own_ref.rest_0_, bf16[4,8192]{1,0:T(4,128)(2,1)S(1)} %collective-permute-done.3.rest_1_, ...), custom_call_target="tpu_custom_call" | custom-call | flops 872415232 | bytes 3788800 | tf_op jit(solution)/shard_map/pallas_call | solution.py:170
  25.6 0.4 %collective-permute-done.9.rest_3_ = bf16[4,8192]{1,0:T(4,128)(2,1)S(1)} collective-permute-done((bf16[4,8192]{1,0:T(4,128)(2,1)S(1)}, bf16[4,8192]{1,0:T(4,128)(2,1)S(1)}, u32[]{:S(2)}, u32[]{:S(2)}) %collective-permute-start.9) | collective-permute-done | bytes 65568 | tf_op jit(solution)/shard_map/ppermute | solution.py:184
  25.9 0.9 %shard_map.32 = (f32[50,128]{1,0:T(8,128)S(1)}, f32[50,128]{1,0:T(8,128)S(1)}, f32[50,128]{1,0:T(8,128)S(1)}, f32[50,128]{1,0:T(8,128)S(1)}) custom-call(bf16[8192,208]{1,0:T(8,128)(2,1)S(1)} %get-tuple-element.20.by_pixel_ref, bf16[4,8192]{1,0:T(4,128)(2,1)S(1)} %shard_map.30.own_ref.rest_0_, f32[64,208]{1,0:T(8,128)S(1)} %shard_map.31.first_ref, ...), custom_call_target="tpu_custom_call" | custom-call | flops 872415232 | bytes 3891200 | tf_op jit(solution)/shard_map/pallas_call | solution.py:170
  26.8 1.5 %collective-permute-start.10 = (f32[50,128]{1,0:T(8,128)S(1)}, f32[50,128]{1,0:T(8,128)S(1)}, u32[]{:S(2)}, u32[]{:S(2)}) collective-permute-start(f32[50,128]{1,0:T(8,128)S(1)} %get-tuple-element.24), channel_id=1, source_target_pairs={{0,8},{8,0},{16,24},{24,16},{1,9},{9,1},{17,25},{25,17},{2,10},{10... | collective-permute-start | bytes 76808 | tf_op jit(solution)/shard_map/ppermute | solution.py:184
  28.4 0.7 %collective-permute-start.11 = (f32[50,128]{1,0:T(8,128)S(1)}, f32[50,128]{1,0:T(8,128)S(1)}, u32[]{:S(2)}, u32[]{:S(2)}) collective-permute-start(f32[50,128]{1,0:T(8,128)S(1)} %get-tuple-element.25), channel_id=1, source_target_pairs={{0,24},{8,16},{16,8},{24,0},{1,25},{9,17},{17,9},{25,1},{2,26},{10... | collective-permute-start | bytes 76808 | tf_op jit(solution)/shard_map/ppermute | solution.py:184
  29.0 1.4 %collective-permute-start.12 = (f32[50,128]{1,0:T(8,128)S(1)}, f32[50,128]{1,0:T(8,128)S(1)}, u32[]{:S(2)}, u32[]{:S(2)}) collective-permute-start(f32[50,128]{1,0:T(8,128)S(1)} %get-tuple-element.26), channel_id=1, source_target_pairs={{0,16},{8,24},{16,0},{24,8},{1,17},{9,25},{17,1},{25,9},{2,18},{10... | collective-permute-start | bytes 76808 | tf_op jit(solution)/shard_map/ppermute | solution.py:184
  30.4 0.4 %collective-permute-done.10.rest_1_ = f32[50,128]{1,0:T(8,128)S(1)} collective-permute-done((f32[50,128]{1,0:T(8,128)S(1)}, f32[50,128]{1,0:T(8,128)S(1)}, u32[]{:S(2)}, u32[]{:S(2)}) %collective-permute-start.10) | collective-permute-done | bytes 25632 | tf_op jit(solution)/shard_map/ppermute | solution.py:184
  30.8 2.4 %collective-permute-done.11.rest_2_ = f32[50,128]{1,0:T(8,128)S(1)} collective-permute-done((f32[50,128]{1,0:T(8,128)S(1)}, f32[50,128]{1,0:T(8,128)S(1)}, u32[]{:S(2)}, u32[]{:S(2)}) %collective-permute-start.11) | collective-permute-done | bytes 25632 | tf_op jit(solution)/shard_map/ppermute | solution.py:184
  33.2 0.9 %shard_map.33 = f32[128,50]{1,0:T(8,128)} custom-call(f32[208,128]{1,0:T(8,128)S(1)} %get-tuple-element.19.counts_ref, f32[50,128]{1,0:T(8,128)S(1)} %get-tuple-element.23.rest_0_, f32[50,128]{1,0:T(8,128)S(1)} %collective-permute-done.10.rest_1_, f32[50,128]{1,0:T(8,128)S(1)} %collective-permute-done.11.rest_2_, f32[50,128]{1,0:T(8,128)S(1)} %collective-permute-done.12.rest_3_), custom_call_target="tpu_custom_call" | custom-call | flops 13631488 | bytes 234496 | tf_op jit(solution)/shard_map/pallas_call | solution.py:170
  (8 shorter events, 0.0 us)
Async XLA Ops:
  2.7 6.6 %collective-permute-start = (f32[200,128]{1,0:T(8,128)S(1)}, f32[200,128]{1,0:T(8,128)S(1)}, u32[]{:S(2)}, u32[]{:S(2)}) collective-permute-start(f32[200,128]{1,0:T(8,128)S(1)} %get-tuple-element.22.own_ref), channel_id=1, source_target_pairs={{0,8},{8,0},{16,24},{24,16},{1,9},{9,1},{17,25},{25,17},{2,10},{10... | collective-permute-start | bytes 307208 | tf_op jit(solution)/shard_map/ppermute | solution.py:184
  5.7 6.4 %collective-permute-start.1 = (f32[200,128]{1,0:T(8,128)S(1)}, f32[200,128]{1,0:T(8,128)S(1)}, u32[]{:S(2)}, u32[]{:S(2)}) collective-permute-start(f32[200,128]{1,0:T(8,128)S(1)} %get-tuple-element.22.own_ref), channel_id=1, source_target_pairs={{0,24},{8,16},{16,8},{24,0},{1,25},{9,17},{17,9},{25,1},{2,26},{10... | collective-permute-start | bytes 307208 | tf_op jit(solution)/shard_map/ppermute | solution.py:184
  7.2 6.1 %collective-permute-start.2 = (f32[200,128]{1,0:T(8,128)S(1)}, f32[200,128]{1,0:T(8,128)S(1)}, u32[]{:S(2)}, u32[]{:S(2)}) collective-permute-start(f32[200,128]{1,0:T(8,128)S(1)} %get-tuple-element.22.own_ref), channel_id=1, source_target_pairs={{0,16},{8,24},{16,0},{24,8},{1,17},{9,25},{17,1},{25,9},{2,18},{10... | collective-permute-start | bytes 307208 | tf_op jit(solution)/shard_map/ppermute | solution.py:184
  14.7 4.3 %collective-permute-start.3 = (bf16[4,8192]{1,0:T(4,128)(2,1)S(1)}, bf16[4,8192]{1,0:T(4,128)(2,1)S(1)}, u32[]{:S(2)}, u32[]{:S(2)}) collective-permute-start(bf16[4,8192]{1,0:T(4,128)(2,1)S(1)} %shard_map.30.own_ref.rest_0_), channel_id=1, source_target_pairs={{0,2},{1,3},{2,0},{3,1},{4,6},{5,7},{6,4},{7,5},{8,10},{9,11},{10,... | collective-permute-start | bytes 196616 | tf_op jit(solution)/shard_map/ppermute | solution.py:184
  16.3 6.2 %collective-permute-start.4 = (bf16[4,8192]{1,0:T(4,128)(2,1)S(1)}, bf16[4,8192]{1,0:T(4,128)(2,1)S(1)}, u32[]{:S(2)}, u32[]{:S(2)}) collective-permute-start(bf16[4,8192]{1,0:T(4,128)(2,1)S(1)} %shard_map.30.own_ref.rest_0_), channel_id=1, source_target_pairs={{0,6},{1,7},{2,4},{3,5},{4,2},{5,3},{6,0},{7,1},{8,14},{9,15},{10,... | collective-permute-start | bytes 196616 | tf_op jit(solution)/shard_map/ppermute | solution.py:184
  18.8 5.9 %collective-permute-start.5 = (bf16[4,8192]{1,0:T(4,128)(2,1)S(1)}, bf16[4,8192]{1,0:T(4,128)(2,1)S(1)}, u32[]{:S(2)}, u32[]{:S(2)}) collective-permute-start(bf16[4,8192]{1,0:T(4,128)(2,1)S(1)} %shard_map.30.own_ref.rest_0_), channel_id=1, source_target_pairs={{0,4},{1,5},{2,6},{3,7},{4,0},{5,1},{6,2},{7,3},{8,12},{9,13},{10,... | collective-permute-start | bytes 196616 | tf_op jit(solution)/shard_map/ppermute | solution.py:184
  18.9 6.6 %collective-permute-start.6 = (bf16[4,8192]{1,0:T(4,128)(2,1)S(1)}, bf16[4,8192]{1,0:T(4,128)(2,1)S(1)}, u32[]{:S(2)}, u32[]{:S(2)}) collective-permute-start(bf16[4,8192]{1,0:T(4,128)(2,1)S(1)} %shard_map.30.own_ref.rest_0_), channel_id=1, source_target_pairs={{0,1},{1,0},{2,3},{3,2},{4,5},{5,4},{6,7},{7,6},{8,9},{9,8},{10,11... | collective-permute-start | bytes 196616 | tf_op jit(solution)/shard_map/ppermute | solution.py:184
  19.0 6.5 %collective-permute-start.7 = (bf16[4,8192]{1,0:T(4,128)(2,1)S(1)}, bf16[4,8192]{1,0:T(4,128)(2,1)S(1)}, u32[]{:S(2)}, u32[]{:S(2)}) collective-permute-start(bf16[4,8192]{1,0:T(4,128)(2,1)S(1)} %collective-permute-done.3.rest_1_), channel_id=1, source_target_pairs={{0,1},{1,0},{2,3},{3,2},{4,5},{5,4},{6,7},{7,6},{8,9},{9,8},{10,11... | collective-permute-start | bytes 196616 | tf_op jit(solution)/shard_map/ppermute | solution.py:184
  22.5 3.0 %collective-permute-start.8 = (bf16[4,8192]{1,0:T(4,128)(2,1)S(1)}, bf16[4,8192]{1,0:T(4,128)(2,1)S(1)}, u32[]{:S(2)}, u32[]{:S(2)}) collective-permute-start(bf16[4,8192]{1,0:T(4,128)(2,1)S(1)} %collective-permute-done.4.rest_2_), channel_id=1, source_target_pairs={{0,1},{1,0},{2,3},{3,2},{4,5},{5,4},{6,7},{7,6},{8,9},{9,8},{10,11... | collective-permute-start | bytes 196616 | tf_op jit(solution)/shard_map/ppermute | solution.py:184
  24.7 1.3 %collective-permute-start.9 = (bf16[4,8192]{1,0:T(4,128)(2,1)S(1)}, bf16[4,8192]{1,0:T(4,128)(2,1)S(1)}, u32[]{:S(2)}, u32[]{:S(2)}) collective-permute-start(bf16[4,8192]{1,0:T(4,128)(2,1)S(1)} %collective-permute-done.5.rest_3_), channel_id=1, source_target_pairs={{0,1},{1,0},{2,3},{3,2},{4,5},{5,4},{6,7},{7,6},{8,9},{9,8},{10,11... | collective-permute-start | bytes 196616 | tf_op jit(solution)/shard_map/ppermute | solution.py:184
  26.8 3.9 %collective-permute-start.10 = (f32[50,128]{1,0:T(8,128)S(1)}, f32[50,128]{1,0:T(8,128)S(1)}, u32[]{:S(2)}, u32[]{:S(2)}) collective-permute-start(f32[50,128]{1,0:T(8,128)S(1)} %get-tuple-element.24), channel_id=1, source_target_pairs={{0,8},{8,0},{16,24},{24,16},{1,9},{9,1},{17,25},{25,17},{2,10},{10... | collective-permute-start | bytes 76808 | tf_op jit(solution)/shard_map/ppermute | solution.py:184
  28.4 4.9 %collective-permute-start.11 = (f32[50,128]{1,0:T(8,128)S(1)}, f32[50,128]{1,0:T(8,128)S(1)}, u32[]{:S(2)}, u32[]{:S(2)}) collective-permute-start(f32[50,128]{1,0:T(8,128)S(1)} %get-tuple-element.25), channel_id=1, source_target_pairs={{0,24},{8,16},{16,8},{24,0},{1,25},{9,17},{17,9},{25,1},{2,26},{10... | collective-permute-start | bytes 76808 | tf_op jit(solution)/shard_map/ppermute | solution.py:184
  29.0 4.2 %collective-permute-start.12 = (f32[50,128]{1,0:T(8,128)S(1)}, f32[50,128]{1,0:T(8,128)S(1)}, u32[]{:S(2)}, u32[]{:S(2)}) collective-permute-start(f32[50,128]{1,0:T(8,128)S(1)} %get-tuple-element.26), channel_id=1, source_target_pairs={{0,16},{8,24},{16,0},{24,8},{1,17},{9,25},{17,1},{25,9},{2,18},{10... | collective-permute-start | bytes 76808 | tf_op jit(solution)/shard_map/ppermute | solution.py:184

commit v3 on v2

--- a/solution.py
+++ b/solution.py
@@ -1,4 +1,5 @@
 import functools
+import math
 
 import jax
 import jax.numpy as jnp
@@ -10,6 +11,8 @@
 NBINS = 200
 TBIN = 4
 GROUP = 8
+MAX_INTENSITY = 820.0
+MAX_HALF = 65504.0
 F32 = jnp.float32
 BF16 = jnp.bfloat16
 NT = (((1,), (1,)), ((), ()))
@@ -193,7 +196,7 @@
     shape = jax.ShapeDtypeStruct
     flops = 2 * rows * pixels * 256
 
-    mod_order = (1, 3, 2) if n_mod == 4 else tuple(range(1, n_mod))
+    mod_order = tuple(range(1, n_mod))
     partial, onehot, kept, bins = call(
         functools.partial(totals_kernel, chunk=chunk),
         [
@@ -207,7 +210,9 @@
         flops=flops, in_specs=[HBM, HBM],
         scratch=[pltpu.SemaphoreType.DMA, pltpu.SemaphoreType.DMA],
     )
-    others = [swap(partial, "mod", s) for s in mod_order]
+    scale = 2.0 ** math.ceil(math.log2(MAX_INTENSITY * pixels / MAX_HALF))
+    sent = (partial * (1.0 / scale)).astype(jnp.float16)
+    others = [swap(sent, "mod", s).astype(F32) * scale for s in mod_order]
     counts, flipped, by_pixel = call(
         functools.partial(prepare_kernel, chunk=chunk),
         [shape((rows, 128), F32), shape((frames, pixels), F32), shape((pixels, rows), BF16)],

time: 34.2 us -> 32.7 us (0.956)
  waiting for transfers between devices: 12.5 us -> 11.3 us
    ppermute x13, waiting for transfers between devices: 12.5 us -> 11.3 us  [swap(): return lax.ppermute(value, axis, [(i, i ^ distance) for i in range(size)])]
    ppermute x13, starting transfers between devices: 12.7 us -> 12.4 us  [swap(): return lax.ppermute(value, axis, [(i, i ^ distance) for i in range(size)])]
  transfers between devices with their start and end apart: 13 -> 13, of which waited for: 8 -> 9; matrix products, arithmetic and copies ran while one was open for 0% -> 0% of each run, Pallas kernels for 9% -> 9%
where the time goes in v3:
time: 32.7 us; the launch traced here: 32.6 us
  starting transfers between devices  12.4 us (38%)
  waiting for transfers between devices  11.3 us (35%)
  Pallas kernels  8.78 us (27%)
    ppermute x13, starting transfers between devices, swap(): return lax.ppermute(value, axis, [(i, i ^ distance) for i in range(size)])  12.4 us
    ppermute x13, waiting for transfers between devices, swap(): return lax.ppermute(value, axis, [(i, i ^ distance) for i in range(size)])  11.3 us
    pallas_call x6, Pallas kernels, call(): pl.pallas_call(kernel, out_shape=tuple(outs), in_specs=in_specs or [VMEM]...  8.78 us
  transfers between devices with their start and end apart: 13, of which 9 were waited for; matrix products, arithmetic and copies ran while one was open for 0% of the time, Pallas kernels for 9%

profile of v3, /device:TPU:0, one launch (start us, length us, event | category | flops | bytes accessed | tf_op | source)
XLA Modules:
  0.0 32.6 jit_solution(2076413727434483190)
XLA Ops:
  0.0 2.7 %shard_map.28 = (f32[200,128]{1,0:T(8,128)S(1)}, bf16[208,8192]{1,0:T(8,128)(2,1)S(1)}, bf16[8192,128]{1,0:T(8,128)(2,1)S(1)}, s32[4,1,8192]{2,1,0:T(1,128)S(1)}) custom-call(s32[4,1,8192]{2,1,0:T(1,128)} %bitcast.4, bf16[8192,128]{1,0:T(8,128)(2,1)} %intensity_hbm.1), custom_call_target="tpu_custom_call" | custom-call | flops 872415232 | bytes 7966720 | tf_op jit(solution)/shard_map/pallas_call | solution.py:173
  2.8 4.0 %collective-permute-start.2 = (f16[200,128]{1,0:T(8,128)(2,1)S(1)}, f16[200,128]{1,0:T(8,128)(2,1)S(1)}, u32[]{:S(2)}, u32[]{:S(2)}) collective-permute-start(f16[200,128]{1,0:T(8,128)(2,1)S(1)} %multiply_convert_fusion), channel_id=1, source_target_pairs={{0,24},{8,16},{16,8},{24,0},{1,25},{9,17},{17,9},{25,1},{2,26},{10... | collective-permute-start | bytes 153608 | tf_op jit(solution)/shard_map/ppermute | solution.py:187
  6.7 0.5 %collective-permute-start.1 = (f16[200,128]{1,0:T(8,128)(2,1)S(1)}, f16[200,128]{1,0:T(8,128)(2,1)S(1)}, u32[]{:S(2)}, u32[]{:S(2)}) collective-permute-start(f16[200,128]{1,0:T(8,128)(2,1)S(1)} %multiply_convert_fusion), channel_id=1, source_target_pairs={{0,16},{8,24},{16,0},{24,8},{1,17},{9,25},{17,1},{25,9},{2,18},{10... | collective-permute-start | bytes 153608 | tf_op jit(solution)/shard_map/ppermute | solution.py:187
  7.2 0.1 collective-permute-start
  7.4 2.1 %shard_map.29 = (f32[208,128]{1,0:T(8,128)S(1)}, f32[128,8192]{1,0:T(8,128)S(1)}, bf16[8192,208]{1,0:T(8,128)(2,1)S(1)}) custom-call(s32[4,1,8192]{2,1,0:T(1,128)S(1)} %get-tuple-element.16.bins_ref, bf16[8192,128]{1,0:T(8,128)(2,1)S(1)} %get-tuple-element.17.intensity_ref, bf16[208,8192]{1,0:T(8,128)(2,1)S(1)} %get-tuple-element.18.onehot_ref), custom_call_target="tpu_custom_call" | custom-call | flops 872415232 | bytes 13344768 | tf_op jit(solution)/shard_map/pallas_call | solution.py:173
  9.5 1.3 %collective-permute-done.1 = f16[200,128]{1,0:T(8,128)(2,1)S(1)} collective-permute-done((f16[200,128]{1,0:T(8,128)(2,1)S(1)}, f16[200,128]{1,0:T(8,128)(2,1)S(1)}, u32[]{:S(2)}, u32[]{:S(2)}) %collective-permute-start.1) | collective-permute-done | bytes 51232 | tf_op jit(solution)/shard_map/ppermute | solution.py:187
  10.8 0.5 %collective-permute-done = f16[200,128]{1,0:T(8,128)(2,1)S(1)} collective-permute-done((f16[200,128]{1,0:T(8,128)(2,1)S(1)}, f16[200,128]{1,0:T(8,128)(2,1)S(1)}, u32[]{:S(2)}, u32[]{:S(2)}) %collective-permute-start) | collective-permute-done | bytes 51232 | tf_op jit(solution)/shard_map/ppermute | solution.py:187
  11.3 1.3 %shard_map.30.own_ref.rest_0_ = bf16[4,8192]{1,0:T(4,128)(2,1)S(1)} custom-call(f32[208,128]{1,0:T(8,128)S(1)} %get-tuple-element.19.counts_ref, bf16[208,8192]{1,0:T(8,128)(2,1)S(1)} %get-tuple-element.18.onehot_ref, f32[128,8192]{1,0:T(8,128)S(1)} %get-tuple-element.21.flipped_ref, f32[200,128]{1,0:T(8,128)S(1)} %get-tuple-element.22.own_ref, ...), custom_call_target="tpu_custom_call" | custom-call | flops 872415232 | bytes 8183808 | tf_op jit(solution)/shard_map/pallas_call | solution.py:173
  12.7 1.6 %collective-permute-start.3 = (bf16[4,8192]{1,0:T(4,128)(2,1)S(1)}, bf16[4,8192]{1,0:T(4,128)(2,1)S(1)}, u32[]{:S(2)}, u32[]{:S(2)}) collective-permute-start(bf16[4,8192]{1,0:T(4,128)(2,1)S(1)} %shard_map.30.own_ref.rest_0_), channel_id=1, source_target_pairs={{0,2},{1,3},{2,0},{3,1},{4,6},{5,7},{6,4},{7,5},{8,10},{9,11},{10,... | collective-permute-start | bytes 196616 | tf_op jit(solution)/shard_map/ppermute | solution.py:187
  14.3 2.5 %collective-permute-start.4 = (bf16[4,8192]{1,0:T(4,128)(2,1)S(1)}, bf16[4,8192]{1,0:T(4,128)(2,1)S(1)}, u32[]{:S(2)}, u32[]{:S(2)}) collective-permute-start(bf16[4,8192]{1,0:T(4,128)(2,1)S(1)} %shard_map.30.own_ref.rest_0_), channel_id=1, source_target_pairs={{0,6},{1,7},{2,4},{3,5},{4,2},{5,3},{6,0},{7,1},{8,14},{9,15},{10,... | collective-permute-start | bytes 196616 | tf_op jit(solution)/shard_map/ppermute | solution.py:187
  16.8 0.1 collective-permute-start.5
  16.9 0.8 %collective-permute-done.3.rest_1_ = bf16[4,8192]{1,0:T(4,128)(2,1)S(1)} collective-permute-done((bf16[4,8192]{1,0:T(4,128)(2,1)S(1)}, bf16[4,8192]{1,0:T(4,128)(2,1)S(1)}, u32[]{:S(2)}, u32[]{:S(2)}) %collective-permute-start.3) | collective-permute-done | bytes 65568 | tf_op jit(solution)/shard_map/ppermute | solution.py:187
  17.7 2.7 %collective-permute-done.4.rest_2_ = bf16[4,8192]{1,0:T(4,128)(2,1)S(1)} collective-permute-done((bf16[4,8192]{1,0:T(4,128)(2,1)S(1)}, bf16[4,8192]{1,0:T(4,128)(2,1)S(1)}, u32[]{:S(2)}, u32[]{:S(2)}) %collective-permute-start.4) | collective-permute-done | bytes 65568 | tf_op jit(solution)/shard_map/ppermute | solution.py:187
  20.4 2.3 %collective-permute-done.5.rest_3_ = bf16[4,8192]{1,0:T(4,128)(2,1)S(1)} collective-permute-done((bf16[4,8192]{1,0:T(4,128)(2,1)S(1)}, bf16[4,8192]{1,0:T(4,128)(2,1)S(1)}, u32[]{:S(2)}, u32[]{:S(2)}) %collective-permute-start.5) | collective-permute-done | bytes 65568 | tf_op jit(solution)/shard_map/ppermute | solution.py:187
  22.7 0.9 %shard_map.31.first_ref = f32[64,208]{1,0:T(8,128)S(1)} custom-call(bf16[8192,208]{1,0:T(8,128)(2,1)S(1)} %get-tuple-element.20.by_pixel_ref, bf16[4,8192]{1,0:T(4,128)(2,1)S(1)} %shard_map.30.own_ref.rest_0_, bf16[4,8192]{1,0:T(4,128)(2,1)S(1)} %shard_map.30.own_ref.rest_0_, bf16[4,8192]{1,0:T(4,128)(2,1)S(1)} %collective-permute-done.3.rest_1_, ...), custom_call_target="tpu_custom_call" | custom-call | flops 872415232 | bytes 3788800 | tf_op jit(solution)/shard_map/pallas_call | solution.py:173
  23.6 0.4 %collective-permute-done.9.rest_3_ = bf16[4,8192]{1,0:T(4,128)(2,1)S(1)} collective-permute-done((bf16[4,8192]{1,0:T(4,128)(2,1)S(1)}, bf16[4,8192]{1,0:T(4,128)(2,1)S(1)}, u32[]{:S(2)}, u32[]{:S(2)}) %collective-permute-start.9) | collective-permute-done | bytes 65568 | tf_op jit(solution)/shard_map/ppermute | solution.py:187
  23.9 0.9 %shard_map.32 = (f32[50,128]{1,0:T(8,128)S(1)}, f32[50,128]{1,0:T(8,128)S(1)}, f32[50,128]{1,0:T(8,128)S(1)}, f32[50,128]{1,0:T(8,128)S(1)}) custom-call(bf16[8192,208]{1,0:T(8,128)(2,1)S(1)} %get-tuple-element.20.by_pixel_ref, bf16[4,8192]{1,0:T(4,128)(2,1)S(1)} %shard_map.30.own_ref.rest_0_, f32[64,208]{1,0:T(8,128)S(1)} %shard_map.31.first_ref, ...), custom_call_target="tpu_custom_call" | custom-call | flops 872415232 | bytes 3891200 | tf_op jit(solution)/shard_map/pallas_call | solution.py:173
  24.9 0.6 %collective-permute-start.10 = (f32[50,128]{1,0:T(8,128)S(1)}, f32[50,128]{1,0:T(8,128)S(1)}, u32[]{:S(2)}, u32[]{:S(2)}) collective-permute-start(f32[50,128]{1,0:T(8,128)S(1)} %get-tuple-element.24), channel_id=1, source_target_pairs={{0,8},{8,0},{16,24},{24,16},{1,9},{9,1},{17,25},{25,17},{2,10},{10... | collective-permute-start | bytes 76808 | tf_op jit(solution)/shard_map/ppermute | solution.py:187
  25.5 1.5 %collective-permute-start.11 = (f32[50,128]{1,0:T(8,128)S(1)}, f32[50,128]{1,0:T(8,128)S(1)}, u32[]{:S(2)}, u32[]{:S(2)}) collective-permute-start(f32[50,128]{1,0:T(8,128)S(1)} %get-tuple-element.25), channel_id=1, source_target_pairs={{0,16},{8,24},{16,0},{24,8},{1,17},{9,25},{17,1},{25,9},{2,18},{10... | collective-permute-start | bytes 76808 | tf_op jit(solution)/shard_map/ppermute | solution.py:187
  27.0 1.4 %collective-permute-start.12 = (f32[50,128]{1,0:T(8,128)S(1)}, f32[50,128]{1,0:T(8,128)S(1)}, u32[]{:S(2)}, u32[]{:S(2)}) collective-permute-start(f32[50,128]{1,0:T(8,128)S(1)} %get-tuple-element.26), channel_id=1, source_target_pairs={{0,24},{8,16},{16,8},{24,0},{1,25},{9,17},{17,9},{25,1},{2,26},{10... | collective-permute-start | bytes 76808 | tf_op jit(solution)/shard_map/ppermute | solution.py:187
  28.4 0.4 %collective-permute-done.10.rest_1_ = f32[50,128]{1,0:T(8,128)S(1)} collective-permute-done((f32[50,128]{1,0:T(8,128)S(1)}, f32[50,128]{1,0:T(8,128)S(1)}, u32[]{:S(2)}, u32[]{:S(2)}) %collective-permute-start.10) | collective-permute-done | bytes 25632 | tf_op jit(solution)/shard_map/ppermute | solution.py:187
  28.8 0.5 %collective-permute-done.11.rest_2_ = f32[50,128]{1,0:T(8,128)S(1)} collective-permute-done((f32[50,128]{1,0:T(8,128)S(1)}, f32[50,128]{1,0:T(8,128)S(1)}, u32[]{:S(2)}, u32[]{:S(2)}) %collective-permute-start.11) | collective-permute-done | bytes 25632 | tf_op jit(solution)/shard_map/ppermute | solution.py:187
  29.3 2.4 %collective-permute-done.12.rest_3_ = f32[50,128]{1,0:T(8,128)S(1)} collective-permute-done((f32[50,128]{1,0:T(8,128)S(1)}, f32[50,128]{1,0:T(8,128)S(1)}, u32[]{:S(2)}, u32[]{:S(2)}) %collective-permute-start.12) | collective-permute-done | bytes 25632 | tf_op jit(solution)/shard_map/ppermute | solution.py:187
  31.8 0.9 %shard_map.33 = f32[128,50]{1,0:T(8,128)} custom-call(f32[208,128]{1,0:T(8,128)S(1)} %get-tuple-element.19.counts_ref, f32[50,128]{1,0:T(8,128)S(1)} %get-tuple-element.23.rest_0_, f32[50,128]{1,0:T(8,128)S(1)} %collective-permute-done.10.rest_1_, f32[50,128]{1,0:T(8,128)S(1)} %collective-permute-done.11.rest_2_, f32[50,128]{1,0:T(8,128)S(1)} %collective-permute-done.12.rest_3_), custom_call_target="tpu_custom_call" | custom-call | flops 13631488 | bytes 234496 | tf_op jit(solution)/shard_map/pallas_call | solution.py:173
  (12 shorter events, 0.1 us)
Async XLA Ops:
  2.8 6.7 %collective-permute-start.2 = (f16[200,128]{1,0:T(8,128)(2,1)S(1)}, f16[200,128]{1,0:T(8,128)(2,1)S(1)}, u32[]{:S(2)}, u32[]{:S(2)}) collective-permute-start(f16[200,128]{1,0:T(8,128)(2,1)S(1)} %multiply_convert_fusion), channel_id=1, source_target_pairs={{0,24},{8,16},{16,8},{24,0},{1,25},{9,17},{17,9},{25,1},{2,26},{10... | collective-permute-start | bytes 153608 | tf_op jit(solution)/shard_map/ppermute | solution.py:187
  6.7 4.1 %collective-permute-start.1 = (f16[200,128]{1,0:T(8,128)(2,1)S(1)}, f16[200,128]{1,0:T(8,128)(2,1)S(1)}, u32[]{:S(2)}, u32[]{:S(2)}) collective-permute-start(f16[200,128]{1,0:T(8,128)(2,1)S(1)} %multiply_convert_fusion), channel_id=1, source_target_pairs={{0,16},{8,24},{16,0},{24,8},{1,17},{9,25},{17,1},{25,9},{2,18},{10... | collective-permute-start | bytes 153608 | tf_op jit(solution)/shard_map/ppermute | solution.py:187
  7.2 4.1 %collective-permute-start = (f16[200,128]{1,0:T(8,128)(2,1)S(1)}, f16[200,128]{1,0:T(8,128)(2,1)S(1)}, u32[]{:S(2)}, u32[]{:S(2)}) collective-permute-start(f16[200,128]{1,0:T(8,128)(2,1)S(1)} %multiply_convert_fusion), channel_id=1, source_target_pairs={{0,8},{8,0},{16,24},{24,16},{1,9},{9,1},{17,25},{25,17},{2,10},{10... | collective-permute-start | bytes 153608 | tf_op jit(solution)/shard_map/ppermute | solution.py:187
  12.7 5.0 %collective-permute-start.3 = (bf16[4,8192]{1,0:T(4,128)(2,1)S(1)}, bf16[4,8192]{1,0:T(4,128)(2,1)S(1)}, u32[]{:S(2)}, u32[]{:S(2)}) collective-permute-start(bf16[4,8192]{1,0:T(4,128)(2,1)S(1)} %shard_map.30.own_ref.rest_0_), channel_id=1, source_target_pairs={{0,2},{1,3},{2,0},{3,1},{4,6},{5,7},{6,4},{7,5},{8,10},{9,11},{10,... | collective-permute-start | bytes 196616 | tf_op jit(solution)/shard_map/ppermute | solution.py:187
  14.3 6.1 %collective-permute-start.4 = (bf16[4,8192]{1,0:T(4,128)(2,1)S(1)}, bf16[4,8192]{1,0:T(4,128)(2,1)S(1)}, u32[]{:S(2)}, u32[]{:S(2)}) collective-permute-start(bf16[4,8192]{1,0:T(4,128)(2,1)S(1)} %shard_map.30.own_ref.rest_0_), channel_id=1, source_target_pairs={{0,6},{1,7},{2,4},{3,5},{4,2},{5,3},{6,0},{7,1},{8,14},{9,15},{10,... | collective-permute-start | bytes 196616 | tf_op jit(solution)/shard_map/ppermute | solution.py:187
  16.8 5.9 %collective-permute-start.5 = (bf16[4,8192]{1,0:T(4,128)(2,1)S(1)}, bf16[4,8192]{1,0:T(4,128)(2,1)S(1)}, u32[]{:S(2)}, u32[]{:S(2)}) collective-permute-start(bf16[4,8192]{1,0:T(4,128)(2,1)S(1)} %shard_map.30.own_ref.rest_0_), channel_id=1, source_target_pairs={{0,4},{1,5},{2,6},{3,7},{4,0},{5,1},{6,2},{7,3},{8,12},{9,13},{10,... | collective-permute-start | bytes 196616 | tf_op jit(solution)/shard_map/ppermute | solution.py:187
  16.9 6.6 %collective-permute-start.6 = (bf16[4,8192]{1,0:T(4,128)(2,1)S(1)}, bf16[4,8192]{1,0:T(4,128)(2,1)S(1)}, u32[]{:S(2)}, u32[]{:S(2)}) collective-permute-start(bf16[4,8192]{1,0:T(4,128)(2,1)S(1)} %shard_map.30.own_ref.rest_0_), channel_id=1, source_target_pairs={{0,1},{1,0},{2,3},{3,2},{4,5},{5,4},{6,7},{7,6},{8,9},{9,8},{10,11... | collective-permute-start | bytes 196616 | tf_op jit(solution)/shard_map/ppermute | solution.py:187
  17.7 5.8 %collective-permute-start.7 = (bf16[4,8192]{1,0:T(4,128)(2,1)S(1)}, bf16[4,8192]{1,0:T(4,128)(2,1)S(1)}, u32[]{:S(2)}, u32[]{:S(2)}) collective-permute-start(bf16[4,8192]{1,0:T(4,128)(2,1)S(1)} %collective-permute-done.3.rest_1_), channel_id=1, source_target_pairs={{0,1},{1,0},{2,3},{3,2},{4,5},{5,4},{6,7},{7,6},{8,9},{9,8},{10,11... | collective-permute-start | bytes 196616 | tf_op jit(solution)/shard_map/ppermute | solution.py:187
  20.4 3.2 %collective-permute-start.8 = (bf16[4,8192]{1,0:T(4,128)(2,1)S(1)}, bf16[4,8192]{1,0:T(4,128)(2,1)S(1)}, u32[]{:S(2)}, u32[]{:S(2)}) collective-permute-start(bf16[4,8192]{1,0:T(4,128)(2,1)S(1)} %collective-permute-done.4.rest_2_), channel_id=1, source_target_pairs={{0,1},{1,0},{2,3},{3,2},{4,5},{5,4},{6,7},{7,6},{8,9},{9,8},{10,11... | collective-permute-start | bytes 196616 | tf_op jit(solution)/shard_map/ppermute | solution.py:187
  22.7 1.3 %collective-permute-start.9 = (bf16[4,8192]{1,0:T(4,128)(2,1)S(1)}, bf16[4,8192]{1,0:T(4,128)(2,1)S(1)}, u32[]{:S(2)}, u32[]{:S(2)}) collective-permute-start(bf16[4,8192]{1,0:T(4,128)(2,1)S(1)} %collective-permute-done.5.rest_3_), channel_id=1, source_target_pairs={{0,1},{1,0},{2,3},{3,2},{4,5},{5,4},{6,7},{7,6},{8,9},{9,8},{10,11... | collective-permute-start | bytes 196616 | tf_op jit(solution)/shard_map/ppermute | solution.py:187
  24.9 3.9 %collective-permute-start.10 = (f32[50,128]{1,0:T(8,128)S(1)}, f32[50,128]{1,0:T(8,128)S(1)}, u32[]{:S(2)}, u32[]{:S(2)}) collective-permute-start(f32[50,128]{1,0:T(8,128)S(1)} %get-tuple-element.24), channel_id=1, source_target_pairs={{0,8},{8,0},{16,24},{24,16},{1,9},{9,1},{17,25},{25,17},{2,10},{10... | collective-permute-start | bytes 76808 | tf_op jit(solution)/shard_map/ppermute | solution.py:187
  25.5 3.9 %collective-permute-start.11 = (f32[50,128]{1,0:T(8,128)S(1)}, f32[50,128]{1,0:T(8,128)S(1)}, u32[]{:S(2)}, u32[]{:S(2)}) collective-permute-start(f32[50,128]{1,0:T(8,128)S(1)} %get-tuple-element.25), channel_id=1, source_target_pairs={{0,16},{8,24},{16,0},{24,8},{1,17},{9,25},{17,1},{25,9},{2,18},{10... | collective-permute-start | bytes 76808 | tf_op jit(solution)/shard_map/ppermute | solution.py:187
  27.0 4.8 %collective-permute-start.12 = (f32[50,128]{1,0:T(8,128)S(1)}, f32[50,128]{1,0:T(8,128)S(1)}, u32[]{:S(2)}, u32[]{:S(2)}) collective-permute-start(f32[50,128]{1,0:T(8,128)S(1)} %get-tuple-element.26), channel_id=1, source_target_pairs={{0,24},{8,16},{16,8},{24,0},{1,25},{9,17},{17,9},{25,1},{2,26},{10... | collective-permute-start | bytes 76808 | tf_op jit(solution)/shard_map/ppermute | solution.py:187

commit v4 on v3

--- a/solution.py
+++ b/solution.py
@@ -55,7 +55,7 @@
 
 
 def prepare_kernel(
-    bins_ref, intensity_ref, onehot_ref, counts_ref, flipped_ref, by_pixel_ref, *, chunk
+    bins_ref, intensity_ref, counts_ref, flipped_ref, *, chunk
 ):
     rows, lanes = counts_ref.shape
     frames = intensity_ref.shape[1]
@@ -83,7 +83,13 @@
         flipped_ref[:, start : start + chunk] = lax.dot_general(
             eye, block, NT, preferred_element_type=F32
         )
-        by_pixel_ref[start : start + chunk, :] = onehot_ref[:, start : start + chunk].T
+
+
+def by_pixel_kernel(onehot_ref, after_ref, out_ref, *, chunk):
+    del after_ref
+    for start in range(0, out_ref.shape[0], chunk):
+        part = slice(start, start + chunk)
+        out_ref[part, :] = onehot_ref[:, part].T
 
 
 def pool_kernel(counts_ref, onehot_ref, flipped_ref, own_ref, *rest, chunk):
@@ -197,6 +203,7 @@
     flops = 2 * rows * pixels * 256
 
     mod_order = tuple(range(1, n_mod))
+    last_order = mod_order[::-1]
     partial, onehot, kept, bins = call(
         functools.partial(totals_kernel, chunk=chunk),
         [
@@ -213,22 +220,26 @@
     scale = 2.0 ** math.ceil(math.log2(MAX_INTENSITY * pixels / MAX_HALF))
     sent = (partial * (1.0 / scale)).astype(jnp.float16)
     others = [swap(sent, "mod", s).astype(F32) * scale for s in mod_order]
-    counts, flipped, by_pixel = call(
+    counts, flipped = call(
         functools.partial(prepare_kernel, chunk=chunk),
-        [shape((rows, 128), F32), shape((frames, pixels), F32), shape((pixels, rows), BF16)],
-        bins, kept, onehot, flops=flops,
+        [shape((rows, 128), F32), shape((frames, pixels), F32)],
+        bins, kept, flops=flops,
     )
     pooled = call(
         functools.partial(pool_kernel, chunk=chunk), [shape((TBIN, pixels), BF16)],
         counts, onehot, flipped, partial, *others, flops=flops,
     )
+    by_pixel = call(
+        functools.partial(by_pixel_kernel, chunk=chunk), [shape((pixels, rows), BF16)],
+        onehot, pooled, flops=flops,
+    )
     width = TBIN * TBIN * GROUP
     if lax.axis_size("blk") == GROUP:
-        far = [swap(pooled, "blk", s) for s in (2, 6, 4)]
+        far = [swap(pooled, "blk", s) for s in (6,2,4)]
         near = swap(pooled, "blk", 1)
         passed = [swap(piece, "blk", 1) for piece in far]
         groups = [([pooled, *far], [near, *passed])]
-        distances = ((0, 2, 6, 4), (1, 3, 7, 5))
+        distances = ((0, 6, 2, 4), (1, 7, 3, 5))
     else:
         every = lax.all_gather(pooled, "blk", axis=0)
         blocks = [every[b] for b in range(every.shape[0])]
@@ -249,7 +260,7 @@
             by_pixel, pooled, first, *second_pieces, flops=flops,
             scratch=[pltpu.VMEM((rows, width), F32)],
         )
-        arrived = [swap(blocks[s], "mod", s) for s in mod_order]
+        arrived = [swap(blocks[s], "mod", s) for s in last_order]
         columns = call(
             functools.partial(final_kernel, distances=distances),
             [shape((width, bins_owned), F32)], counts, blocks[0], *arrived, flops=flops // 64,

time: 32.7 us -> 30.5 us (0.933)
  waiting for transfers between devices: 11.3 us -> 8.01 us
  Pallas kernels: 8.78 us -> 9.62 us
    ppermute x13, waiting for transfers between devices: 11.3 us -> 8.01 us  [swap(): return lax.ppermute(value, axis, [(i, i ^ distance) for i in range(size)])]
    pallas_call x6 -> x7, Pallas kernels: 8.78 us -> 9.62 us  [call(): pl.pallas_call(kernel, out_shape=tuple(outs), in_specs=in_specs or [VMEM]...]
  transfers between devices with their start and end apart: 13 -> 13, of which waited for: 9 -> 9; matrix products, arithmetic and copies ran while one was open for 0% -> 0% of each run, Pallas kernels for 9% -> 13%
where the time goes in v4:
time: 30.5 us; the launch traced here: 30.4 us
  starting transfers between devices  12.6 us (41%)
  Pallas kernels  9.62 us (32%)
  waiting for transfers between devices  8.01 us (26%)
    ppermute x13, starting transfers between devices, swap(): return lax.ppermute(value, axis, [(i, i ^ distance) for i in range(size)])  12.6 us
    pallas_call x7, Pallas kernels, call(): pl.pallas_call(kernel, out_shape=tuple(outs), in_specs=in_specs or [VMEM]...  9.62 us
    ppermute x13, waiting for transfers between devices, swap(): return lax.ppermute(value, axis, [(i, i ^ distance) for i in range(size)])  8.01 us
  transfers between devices with their start and end apart: 13, of which 9 were waited for; matrix products, arithmetic and copies ran while one was open for 0% of the time, Pallas kernels for 13%

profile of v4, /device:TPU:0, one launch (start us, length us, event | category | flops | bytes accessed | tf_op | source)
XLA Modules:
  0.0 30.4 jit_solution(5632190149754438791)
XLA Ops:
  0.0 2.7 %shard_map.28 = (f32[200,128]{1,0:T(8,128)S(1)}, bf16[208,8192]{1,0:T(8,128)(2,1)S(1)}, bf16[8192,128]{1,0:T(8,128)(2,1)S(1)}, s32[4,1,8192]{2,1,0:T(1,128)S(1)}) custom-call(s32[4,1,8192]{2,1,0:T(1,128)} %bitcast.4, bf16[8192,128]{1,0:T(8,128)(2,1)} %intensity_hbm.1), custom_call_target="tpu_custom_call" | custom-call | flops 872415232 | bytes 7966720 | tf_op jit(solution)/shard_map/pallas_call | solution.py:179
  2.8 4.0 %collective-permute-start.2 = (f16[200,128]{1,0:T(8,128)(2,1)S(1)}, f16[200,128]{1,0:T(8,128)(2,1)S(1)}, u32[]{:S(2)}, u32[]{:S(2)}) collective-permute-start(f16[200,128]{1,0:T(8,128)(2,1)S(1)} %multiply_convert_fusion), channel_id=1, source_target_pairs={{0,24},{8,16},{16,8},{24,0},{1,25},{9,17},{17,9},{25,1},{2,26},{10... | collective-permute-start | bytes 153608 | tf_op jit(solution)/shard_map/ppermute | solution.py:193
  6.7 0.5 %collective-permute-start.1 = (f16[200,128]{1,0:T(8,128)(2,1)S(1)}, f16[200,128]{1,0:T(8,128)(2,1)S(1)}, u32[]{:S(2)}, u32[]{:S(2)}) collective-permute-start(f16[200,128]{1,0:T(8,128)(2,1)S(1)} %multiply_convert_fusion), channel_id=1, source_target_pairs={{0,16},{8,24},{16,0},{24,8},{1,17},{9,25},{17,1},{25,9},{2,18},{10... | collective-permute-start | bytes 153608 | tf_op jit(solution)/shard_map/ppermute | solution.py:193
  7.2 0.1 collective-permute-start
  7.4 2.0 %shard_map.29 = (f32[208,128]{1,0:T(8,128)S(1)}, f32[128,8192]{1,0:T(8,128)S(1)}) custom-call(s32[4,1,8192]{2,1,0:T(1,128)S(1)} %get-tuple-element.15.bins_ref, bf16[8192,128]{1,0:T(8,128)(2,1)S(1)} %get-tuple-element.16.intensity_ref), custom_call_target="tpu_custom_call" | custom-call | flops 872415232 | bytes 6529024 | tf_op jit(solution)/shard_map/pallas_call | solution.py:179
  9.4 1.4 %collective-permute-done.1 = f16[200,128]{1,0:T(8,128)(2,1)S(1)} collective-permute-done((f16[200,128]{1,0:T(8,128)(2,1)S(1)}, f16[200,128]{1,0:T(8,128)(2,1)S(1)}, u32[]{:S(2)}, u32[]{:S(2)}) %collective-permute-start.1) | collective-permute-done | bytes 51232 | tf_op jit(solution)/shard_map/ppermute | solution.py:193
  10.8 0.5 %collective-permute-done = f16[200,128]{1,0:T(8,128)(2,1)S(1)} collective-permute-done((f16[200,128]{1,0:T(8,128)(2,1)S(1)}, f16[200,128]{1,0:T(8,128)(2,1)S(1)}, u32[]{:S(2)}, u32[]{:S(2)}) %collective-permute-start) | collective-permute-done | bytes 51232 | tf_op jit(solution)/shard_map/ppermute | solution.py:193
  11.3 1.3 %shard_map.30.after_ref.own_ref.rest_0_ = bf16[4,8192]{1,0:T(4,128)(2,1)S(1)} custom-call(f32[208,128]{1,0:T(8,128)S(1)} %get-tuple-element.17.counts_ref, bf16[208,8192]{1,0:T(8,128)(2,1)S(1)} %get-tuple-element.18.onehot_ref, f32[128,8192]{1,0:T(8,128)S(1)} %get-tuple-element.19.flipped_ref, f32[200,128]{1,0:T(8,128)S(1)} %get-tuple-element.20.own_ref, ...), custom_call_target="tpu_custom_call" | custom-call | flops 872415232 | bytes 8183808 | tf_op jit(solution)/shard_map/pallas_call | solution.py:179
  12.7 3.7 %collective-permute-start.3 = (bf16[4,8192]{1,0:T(4,128)(2,1)S(1)}, bf16[4,8192]{1,0:T(4,128)(2,1)S(1)}, u32[]{:S(2)}, u32[]{:S(2)}) collective-permute-start(bf16[4,8192]{1,0:T(4,128)(2,1)S(1)} %shard_map.30.after_ref.own_ref.rest_0_), channel_id=1, source_target_pairs={{0,6},{1,7},{2,4},{3,5},{4,2},{5,3},{6,0},{7,1},{8,14},{9,15},{10,... | collective-permute-start | bytes 196616 | tf_op jit(solution)/shard_map/ppermute | solution.py:193
  16.4 0.8 %collective-permute-start.5 = (bf16[4,8192]{1,0:T(4,128)(2,1)S(1)}, bf16[4,8192]{1,0:T(4,128)(2,1)S(1)}, u32[]{:S(2)}, u32[]{:S(2)}) collective-permute-start(bf16[4,8192]{1,0:T(4,128)(2,1)S(1)} %shard_map.30.after_ref.own_ref.rest_0_), channel_id=1, source_target_pairs={{0,4},{1,5},{2,6},{3,7},{4,0},{5,1},{6,2},{7,3},{8,12},{9,13},{10,... | collective-permute-start | bytes 196616 | tf_op jit(solution)/shard_map/ppermute | solution.py:193
  17.1 1.2 %shard_map.31.by_pixel_ref = bf16[8192,208]{1,0:T(8,128)(2,1)S(1)} custom-call(bf16[208,8192]{1,0:T(8,128)(2,1)S(1)} %get-tuple-element.18.onehot_ref, bf16[4,8192]{1,0:T(4,128)(2,1)S(1)} %shard_map.30.after_ref.own_ref.rest_0_), custom_call_target="tpu_custom_call" | custom-call | flops 872415232 | bytes 6881280 | tf_op jit(solution)/shard_map/pallas_call | solution.py:179
  18.3 0.6 %collective-permute-done.3.rest_1_ = bf16[4,8192]{1,0:T(4,128)(2,1)S(1)} collective-permute-done((bf16[4,8192]{1,0:T(4,128)(2,1)S(1)}, bf16[4,8192]{1,0:T(4,128)(2,1)S(1)}, u32[]{:S(2)}, u32[]{:S(2)}) %collective-permute-start.3) | collective-permute-done | bytes 65568 | tf_op jit(solution)/shard_map/ppermute | solution.py:193
  18.9 1.7 %collective-permute-done.4.rest_2_ = bf16[4,8192]{1,0:T(4,128)(2,1)S(1)} collective-permute-done((bf16[4,8192]{1,0:T(4,128)(2,1)S(1)}, bf16[4,8192]{1,0:T(4,128)(2,1)S(1)}, u32[]{:S(2)}, u32[]{:S(2)}) %collective-permute-start.4) | collective-permute-done | bytes 65568 | tf_op jit(solution)/shard_map/ppermute | solution.py:193
  20.6 0.9 %collective-permute-done.5.rest_3_ = bf16[4,8192]{1,0:T(4,128)(2,1)S(1)} collective-permute-done((bf16[4,8192]{1,0:T(4,128)(2,1)S(1)}, bf16[4,8192]{1,0:T(4,128)(2,1)S(1)}, u32[]{:S(2)}, u32[]{:S(2)}) %collective-permute-start.5) | collective-permute-done | bytes 65568 | tf_op jit(solution)/shard_map/ppermute | solution.py:193
  21.5 0.7 %shard_map.32.first_ref = f32[64,208]{1,0:T(8,128)S(1)} custom-call(bf16[8192,208]{1,0:T(8,128)(2,1)S(1)} %shard_map.31.by_pixel_ref, bf16[4,8192]{1,0:T(4,128)(2,1)S(1)} %shard_map.30.after_ref.own_ref.rest_0_, bf16[4,8192]{1,0:T(4,128)(2,1)S(1)} %shard_map.30.after_ref.own_ref.rest_0_, bf16[4,8192]{1,0:T(4,128)(2,1)S(1)} %collective-permute-done.3.rest_1_, ...), custom_call_target="tpu_custom_call" | custom-call | flops 872415232 | bytes 3788800 | tf_op jit(solution)/shard_map/pallas_call | solution.py:179
  22.3 0.5 %collective-permute-done.9.rest_3_ = bf16[4,8192]{1,0:T(4,128)(2,1)S(1)} collective-permute-done((bf16[4,8192]{1,0:T(4,128)(2,1)S(1)}, bf16[4,8192]{1,0:T(4,128)(2,1)S(1)}, u32[]{:S(2)}, u32[]{:S(2)}) %collective-permute-start.9) | collective-permute-done | bytes 65568 | tf_op jit(solution)/shard_map/ppermute | solution.py:193
  22.8 0.8 %shard_map.33 = (f32[50,128]{1,0:T(8,128)S(1)}, f32[50,128]{1,0:T(8,128)S(1)}, f32[50,128]{1,0:T(8,128)S(1)}, f32[50,128]{1,0:T(8,128)S(1)}) custom-call(bf16[8192,208]{1,0:T(8,128)(2,1)S(1)} %shard_map.31.by_pixel_ref, bf16[4,8192]{1,0:T(4,128)(2,1)S(1)} %shard_map.30.after_ref.own_ref.rest_0_, f32[64,208]{1,0:T(8,128)S(1)} %shard_map.32.first_ref, ...), custom_call_target="tpu_custom_call" | custom-call | flops 872415232 | bytes 3891200 | tf_op jit(solution)/shard_map/pallas_call | solution.py:179
  23.6 1.6 %collective-permute-start.10 = (f32[50,128]{1,0:T(8,128)S(1)}, f32[50,128]{1,0:T(8,128)S(1)}, u32[]{:S(2)}, u32[]{:S(2)}) collective-permute-start(f32[50,128]{1,0:T(8,128)S(1)} %get-tuple-element.22), channel_id=1, source_target_pairs={{0,24},{8,16},{16,8},{24,0},{1,25},{9,17},{17,9},{25,1},{2,26},{10... | collective-permute-start | bytes 76808 | tf_op jit(solution)/shard_map/ppermute | solution.py:193
  25.2 0.5 %collective-permute-start.11 = (f32[50,128]{1,0:T(8,128)S(1)}, f32[50,128]{1,0:T(8,128)S(1)}, u32[]{:S(2)}, u32[]{:S(2)}) collective-permute-start(f32[50,128]{1,0:T(8,128)S(1)} %get-tuple-element.23), channel_id=1, source_target_pairs={{0,16},{8,24},{16,0},{24,8},{1,17},{9,25},{17,1},{25,9},{2,18},{10... | collective-permute-start | bytes 76808 | tf_op jit(solution)/shard_map/ppermute | solution.py:193
  25.7 1.5 %collective-permute-start.12 = (f32[50,128]{1,0:T(8,128)S(1)}, f32[50,128]{1,0:T(8,128)S(1)}, u32[]{:S(2)}, u32[]{:S(2)}) collective-permute-start(f32[50,128]{1,0:T(8,128)S(1)} %get-tuple-element.24), channel_id=1, source_target_pairs={{0,8},{8,0},{16,24},{24,16},{1,9},{9,1},{17,25},{25,17},{2,10},{10... | collective-permute-start | bytes 76808 | tf_op jit(solution)/shard_map/ppermute | solution.py:193
  27.2 1.3 %collective-permute-done.10.rest_1_ = f32[50,128]{1,0:T(8,128)S(1)} collective-permute-done((f32[50,128]{1,0:T(8,128)S(1)}, f32[50,128]{1,0:T(8,128)S(1)}, u32[]{:S(2)}, u32[]{:S(2)}) %collective-permute-start.10) | collective-permute-done | bytes 25632 | tf_op jit(solution)/shard_map/ppermute | solution.py:193
  28.4 0.6 %collective-permute-done.11.rest_2_ = f32[50,128]{1,0:T(8,128)S(1)} collective-permute-done((f32[50,128]{1,0:T(8,128)S(1)}, f32[50,128]{1,0:T(8,128)S(1)}, u32[]{:S(2)}, u32[]{:S(2)}) %collective-permute-start.11) | collective-permute-done | bytes 25632 | tf_op jit(solution)/shard_map/ppermute | solution.py:193
  29.0 0.5 %collective-permute-done.12.rest_3_ = f32[50,128]{1,0:T(8,128)S(1)} collective-permute-done((f32[50,128]{1,0:T(8,128)S(1)}, f32[50,128]{1,0:T(8,128)S(1)}, u32[]{:S(2)}, u32[]{:S(2)}) %collective-permute-start.12) | collective-permute-done | bytes 25632 | tf_op jit(solution)/shard_map/ppermute | solution.py:193
  29.5 0.9 %shard_map.34 = f32[128,50]{1,0:T(8,128)} custom-call(f32[208,128]{1,0:T(8,128)S(1)} %get-tuple-element.17.counts_ref, f32[50,128]{1,0:T(8,128)S(1)} %get-tuple-element.21.rest_0_, f32[50,128]{1,0:T(8,128)S(1)} %collective-permute-done.10.rest_1_, f32[50,128]{1,0:T(8,128)S(1)} %collective-permute-done.11.rest_2_, f32[50,128]{1,0:T(8,128)S(1)} %collective-permute-done.12.rest_3_), custom_call_target="tpu_custom_call" | custom-call | flops 13631488 | bytes 234496 | tf_op jit(solution)/shard_map/pallas_call | solution.py:179
  (13 shorter events, 0.1 us)
Async XLA Ops:
  2.8 6.6 %collective-permute-start.2 = (f16[200,128]{1,0:T(8,128)(2,1)S(1)}, f16[200,128]{1,0:T(8,128)(2,1)S(1)}, u32[]{:S(2)}, u32[]{:S(2)}) collective-permute-start(f16[200,128]{1,0:T(8,128)(2,1)S(1)} %multiply_convert_fusion), channel_id=1, source_target_pairs={{0,24},{8,16},{16,8},{24,0},{1,25},{9,17},{17,9},{25,1},{2,26},{10... | collective-permute-start | bytes 153608 | tf_op jit(solution)/shard_map/ppermute | solution.py:193
  6.7 4.1 %collective-permute-start.1 = (f16[200,128]{1,0:T(8,128)(2,1)S(1)}, f16[200,128]{1,0:T(8,128)(2,1)S(1)}, u32[]{:S(2)}, u32[]{:S(2)}) collective-permute-start(f16[200,128]{1,0:T(8,128)(2,1)S(1)} %multiply_convert_fusion), channel_id=1, source_target_pairs={{0,16},{8,24},{16,0},{24,8},{1,17},{9,25},{17,1},{25,9},{2,18},{10... | collective-permute-start | bytes 153608 | tf_op jit(solution)/shard_map/ppermute | solution.py:193
  7.2 4.1 %collective-permute-start = (f16[200,128]{1,0:T(8,128)(2,1)S(1)}, f16[200,128]{1,0:T(8,128)(2,1)S(1)}, u32[]{:S(2)}, u32[]{:S(2)}) collective-permute-start(f16[200,128]{1,0:T(8,128)(2,1)S(1)} %multiply_convert_fusion), channel_id=1, source_target_pairs={{0,8},{8,0},{16,24},{24,16},{1,9},{9,1},{17,25},{25,17},{2,10},{10... | collective-permute-start | bytes 153608 | tf_op jit(solution)/shard_map/ppermute | solution.py:193
  12.7 6.2 %collective-permute-start.3 = (bf16[4,8192]{1,0:T(4,128)(2,1)S(1)}, bf16[4,8192]{1,0:T(4,128)(2,1)S(1)}, u32[]{:S(2)}, u32[]{:S(2)}) collective-permute-start(bf16[4,8192]{1,0:T(4,128)(2,1)S(1)} %shard_map.30.after_ref.own_ref.rest_0_), channel_id=1, source_target_pairs={{0,6},{1,7},{2,4},{3,5},{4,2},{5,3},{6,0},{7,1},{8,14},{9,15},{10,... | collective-permute-start | bytes 196616 | tf_op jit(solution)/shard_map/ppermute | solution.py:193
  16.3 4.3 %collective-permute-start.4 = (bf16[4,8192]{1,0:T(4,128)(2,1)S(1)}, bf16[4,8192]{1,0:T(4,128)(2,1)S(1)}, u32[]{:S(2)}, u32[]{:S(2)}) collective-permute-start(bf16[4,8192]{1,0:T(4,128)(2,1)S(1)} %shard_map.30.after_ref.own_ref.rest_0_), channel_id=1, source_target_pairs={{0,2},{1,3},{2,0},{3,1},{4,6},{5,7},{6,4},{7,5},{8,10},{9,11},{10,... | collective-permute-start | bytes 196616 | tf_op jit(solution)/shard_map/ppermute | solution.py:193
  16.4 5.2 %collective-permute-start.5 = (bf16[4,8192]{1,0:T(4,128)(2,1)S(1)}, bf16[4,8192]{1,0:T(4,128)(2,1)S(1)}, u32[]{:S(2)}, u32[]{:S(2)}) collective-permute-start(bf16[4,8192]{1,0:T(4,128)(2,1)S(1)} %shard_map.30.after_ref.own_ref.rest_0_), channel_id=1, source_target_pairs={{0,4},{1,5},{2,6},{3,7},{4,0},{5,1},{6,2},{7,3},{8,12},{9,13},{10,... | collective-permute-start | bytes 196616 | tf_op jit(solution)/shard_map/ppermute | solution.py:193
  17.1 5.1 %collective-permute-start.6 = (bf16[4,8192]{1,0:T(4,128)(2,1)S(1)}, bf16[4,8192]{1,0:T(4,128)(2,1)S(1)}, u32[]{:S(2)}, u32[]{:S(2)}) collective-permute-start(bf16[4,8192]{1,0:T(4,128)(2,1)S(1)} %shard_map.30.after_ref.own_ref.rest_0_), channel_id=1, source_target_pairs={{0,1},{1,0},{2,3},{3,2},{4,5},{5,4},{6,7},{7,6},{8,9},{9,8},{10,11... | collective-permute-start | bytes 196616 | tf_op jit(solution)/shard_map/ppermute | solution.py:193
  18.9 3.4 %collective-permute-start.7 = (bf16[4,8192]{1,0:T(4,128)(2,1)S(1)}, bf16[4,8192]{1,0:T(4,128)(2,1)S(1)}, u32[]{:S(2)}, u32[]{:S(2)}) collective-permute-start(bf16[4,8192]{1,0:T(4,128)(2,1)S(1)} %collective-permute-done.3.rest_1_), channel_id=1, source_target_pairs={{0,1},{1,0},{2,3},{3,2},{4,5},{5,4},{6,7},{7,6},{8,9},{9,8},{10,11... | collective-permute-start | bytes 196616 | tf_op jit(solution)/shard_map/ppermute | solution.py:193
  20.6 1.7 %collective-permute-start.8 = (bf16[4,8192]{1,0:T(4,128)(2,1)S(1)}, bf16[4,8192]{1,0:T(4,128)(2,1)S(1)}, u32[]{:S(2)}, u32[]{:S(2)}) collective-permute-start(bf16[4,8192]{1,0:T(4,128)(2,1)S(1)} %collective-permute-done.4.rest_2_), channel_id=1, source_target_pairs={{0,1},{1,0},{2,3},{3,2},{4,5},{5,4},{6,7},{7,6},{8,9},{9,8},{10,11... | collective-permute-start | bytes 196616 | tf_op jit(solution)/shard_map/ppermute | solution.py:193
  21.5 1.3 %collective-permute-start.9 = (bf16[4,8192]{1,0:T(4,128)(2,1)S(1)}, bf16[4,8192]{1,0:T(4,128)(2,1)S(1)}, u32[]{:S(2)}, u32[]{:S(2)}) collective-permute-start(bf16[4,8192]{1,0:T(4,128)(2,1)S(1)} %collective-permute-done.5.rest_3_), channel_id=1, source_target_pairs={{0,1},{1,0},{2,3},{3,2},{4,5},{5,4},{6,7},{7,6},{8,9},{9,8},{10,11... | collective-permute-start | bytes 196616 | tf_op jit(solution)/shard_map/ppermute | solution.py:193
  23.6 4.8 %collective-permute-start.10 = (f32[50,128]{1,0:T(8,128)S(1)}, f32[50,128]{1,0:T(8,128)S(1)}, u32[]{:S(2)}, u32[]{:S(2)}) collective-permute-start(f32[50,128]{1,0:T(8,128)S(1)} %get-tuple-element.22), channel_id=1, source_target_pairs={{0,24},{8,16},{16,8},{24,0},{1,25},{9,17},{17,9},{25,1},{2,26},{10... | collective-permute-start | bytes 76808 | tf_op jit(solution)/shard_map/ppermute | solution.py:193
  25.2 3.9 %collective-permute-start.11 = (f32[50,128]{1,0:T(8,128)S(1)}, f32[50,128]{1,0:T(8,128)S(1)}, u32[]{:S(2)}, u32[]{:S(2)}) collective-permute-start(f32[50,128]{1,0:T(8,128)S(1)} %get-tuple-element.23), channel_id=1, source_target_pairs={{0,16},{8,24},{16,0},{24,8},{1,17},{9,25},{17,1},{25,9},{2,18},{10... | collective-permute-start | bytes 76808 | tf_op jit(solution)/shard_map/ppermute | solution.py:193
  25.7 3.9 %collective-permute-start.12 = (f32[50,128]{1,0:T(8,128)S(1)}, f32[50,128]{1,0:T(8,128)S(1)}, u32[]{:S(2)}, u32[]{:S(2)}) collective-permute-start(f32[50,128]{1,0:T(8,128)S(1)} %get-tuple-element.24), channel_id=1, source_target_pairs={{0,8},{8,0},{16,24},{24,16},{1,9},{9,1},{17,25},{25,17},{2,10},{10... | collective-permute-start | bytes 76808 | tf_op jit(solution)/shard_map/ppermute | solution.py:193

commit v5 on v4

--- a/solution.py
+++ b/solution.py
@@ -168,9 +168,13 @@
     if pieces * 2 == lax.axis_size("blk"):
         block ^= lax.axis_index("blk")
     place = jnp.where(out_row == i * (TBIN * GROUP) + block * TBIN + row, 1.0, 0.0).astype(F32)
-    out_ref[...] = lax.dot_general(
-        place, total, NT, precision=lax.Precision.HIGHEST, preferred_element_type=F32
-    )
+    place = place.astype(BF16)
+    high = total.astype(BF16)
+    rest = total - high.astype(F32)
+    middle = rest.astype(BF16)
+    low = (rest - middle.astype(F32)).astype(BF16)
+    moved = [lax.dot_general(place, p, NT, preferred_element_type=F32) for p in (high, middle, low)]
+    out_ref[...] = moved[0] + (moved[1] + moved[2])
 
 
 def call(kernel, outs, *args, flops, in_specs=None, out_specs=None, scratch=()):
@@ -226,7 +230,7 @@
         bins, kept, flops=flops,
     )
     pooled = call(
-        functools.partial(pool_kernel, chunk=chunk), [shape((TBIN, pixels), BF16)],
+        functools.partial(pool_kernel, chunk=4 * chunk), [shape((TBIN, pixels), BF16)],
         counts, onehot, flipped, partial, *others, flops=flops,
     )
     by_pixel = call(
@@ -236,7 +240,8 @@
     width = TBIN * TBIN * GROUP
     if lax.axis_size("blk") == GROUP:
         far = [swap(pooled, "blk", s) for s in (6,2,4)]
-        near = swap(pooled, "blk", 1)
+        far[:2] = lax.optimization_barrier((far[0], far[1]))
+        near = swap(lax.optimization_barrier((pooled, far[0]))[0], "blk", 1)
         passed = [swap(piece, "blk", 1) for piece in far]
         groups = [([pooled, *far], [near, *passed])]
         distances = ((0, 6, 2, 4), (1, 7, 3, 5))

time: 30.5 us -> 30.5 us (level)
  waiting for transfers between devices: 8.01 us -> 7.38 us
  starting transfers between devices: 12.6 us -> 13.2 us
    ppermute x13, waiting for transfers between devices: 8.01 us -> 7.38 us  [swap(): return lax.ppermute(value, axis, [(i, i ^ distance) for i in range(size)])]
    ppermute x13, starting transfers between devices: 12.6 us -> 13.2 us  [swap(): return lax.ppermute(value, axis, [(i, i ^ distance) for i in range(size)])]
where the time goes in v5:
time: 30.5 us; the launch traced here: 30.4 us
  starting transfers between devices  13.2 us (43%)
  Pallas kernels  9.59 us (31%)
  waiting for transfers between devices  7.38 us (24%)
    ppermute x13, starting transfers between devices, swap(): return lax.ppermute(value, axis, [(i, i ^ distance) for i in range(size)])  13.2 us
    pallas_call x7, Pallas kernels, call(): pl.pallas_call(kernel, out_shape=tuple(outs), in_specs=in_specs or [VMEM]...  9.59 us
    ppermute x13, waiting for transfers between devices, swap(): return lax.ppermute(value, axis, [(i, i ^ distance) for i in range(size)])  7.38 us
  transfers between devices with their start and end apart: 13, of which 9 were waited for; matrix products, arithmetic and copies ran while one was open for 0% of the time, Pallas kernels for 13%

profile of v5, /device:TPU:0, one launch (start us, length us, event | category | flops | bytes accessed | tf_op | source)
XLA Modules:
  0.0 30.4 jit_solution(13237709892497749785)
XLA Ops:
  0.0 2.7 %shard_map.28 = (f32[200,128]{1,0:T(8,128)S(1)}, bf16[208,8192]{1,0:T(8,128)(2,1)S(1)}, bf16[8192,128]{1,0:T(8,128)(2,1)S(1)}, s32[4,1,8192]{2,1,0:T(1,128)S(1)}) custom-call(s32[4,1,8192]{2,1,0:T(1,128)} %bitcast.4, bf16[8192,128]{1,0:T(8,128)(2,1)} %intensity_hbm.1), custom_call_target="tpu_custom_call" | custom-call | flops 872415232 | bytes 7966720 | tf_op jit(solution)/shard_map/pallas_call | solution.py:183
  2.8 4.0 %collective-permute-start.2 = (f16[200,128]{1,0:T(8,128)(2,1)S(1)}, f16[200,128]{1,0:T(8,128)(2,1)S(1)}, u32[]{:S(2)}, u32[]{:S(2)}) collective-permute-start(f16[200,128]{1,0:T(8,128)(2,1)S(1)} %multiply_convert_fusion), channel_id=1, source_target_pairs={{0,24},{8,16},{16,8},{24,0},{1,25},{9,17},{17,9},{25,1},{2,26},{10... | collective-permute-start | bytes 153608 | tf_op jit(solution)/shard_map/ppermute | solution.py:197
  6.7 0.5 %collective-permute-start.1 = (f16[200,128]{1,0:T(8,128)(2,1)S(1)}, f16[200,128]{1,0:T(8,128)(2,1)S(1)}, u32[]{:S(2)}, u32[]{:S(2)}) collective-permute-start(f16[200,128]{1,0:T(8,128)(2,1)S(1)} %multiply_convert_fusion), channel_id=1, source_target_pairs={{0,16},{8,24},{16,0},{24,8},{1,17},{9,25},{17,1},{25,9},{2,18},{10... | collective-permute-start | bytes 153608 | tf_op jit(solution)/shard_map/ppermute | solution.py:197
  7.4 2.0 %shard_map.29 = (f32[208,128]{1,0:T(8,128)S(1)}, f32[128,8192]{1,0:T(8,128)S(1)}) custom-call(s32[4,1,8192]{2,1,0:T(1,128)S(1)} %get-tuple-element.18.bins_ref, bf16[8192,128]{1,0:T(8,128)(2,1)S(1)} %get-tuple-element.19.intensity_ref), custom_call_target="tpu_custom_call" | custom-call | flops 872415232 | bytes 6529024 | tf_op jit(solution)/shard_map/pallas_call | solution.py:183
  9.4 1.4 %collective-permute-done.1 = f16[200,128]{1,0:T(8,128)(2,1)S(1)} collective-permute-done((f16[200,128]{1,0:T(8,128)(2,1)S(1)}, f16[200,128]{1,0:T(8,128)(2,1)S(1)}, u32[]{:S(2)}, u32[]{:S(2)}) %collective-permute-start.1) | collective-permute-done | bytes 51232 | tf_op jit(solution)/shard_map/ppermute | solution.py:197
  10.8 0.5 %collective-permute-done = f16[200,128]{1,0:T(8,128)(2,1)S(1)} collective-permute-done((f16[200,128]{1,0:T(8,128)(2,1)S(1)}, f16[200,128]{1,0:T(8,128)(2,1)S(1)}, u32[]{:S(2)}, u32[]{:S(2)}) %collective-permute-start) | collective-permute-done | bytes 51232 | tf_op jit(solution)/shard_map/ppermute | solution.py:197
  11.3 1.3 %shard_map.30.after_ref.own_ref.rest_0_ = bf16[4,8192]{1,0:T(4,128)(2,1)S(1)} custom-call(f32[208,128]{1,0:T(8,128)S(1)} %get-tuple-element.20.counts_ref, bf16[208,8192]{1,0:T(8,128)(2,1)S(1)} %get-tuple-element.21.onehot_ref, f32[128,8192]{1,0:T(8,128)S(1)} %get-tuple-element.22.flipped_ref, f32[200,128]{1,0:T(8,128)S(1)} %get-tuple-element.23.own_ref, ...), custom_call_target="tpu_custom_call" | custom-call | flops 872415232 | bytes 8183808 | tf_op jit(solution)/shard_map/pallas_call | solution.py:183
  12.7 3.7 %collective-permute-start.3 = (bf16[4,8192]{1,0:T(4,128)(2,1)S(1)}, bf16[4,8192]{1,0:T(4,128)(2,1)S(1)}, u32[]{:S(2)}, u32[]{:S(2)}) collective-permute-start(bf16[4,8192]{1,0:T(4,128)(2,1)S(1)} %shard_map.30.after_ref.own_ref.rest_0_), channel_id=1, source_target_pairs={{0,6},{1,7},{2,4},{3,5},{4,2},{5,3},{6,0},{7,1},{8,14},{9,15},{10,... | collective-permute-start | bytes 196616 | tf_op jit(solution)/shard_map/ppermute | solution.py:197
  16.4 0.8 %collective-permute-start.5 = (bf16[4,8192]{1,0:T(4,128)(2,1)S(1)}, bf16[4,8192]{1,0:T(4,128)(2,1)S(1)}, u32[]{:S(2)}, u32[]{:S(2)}) collective-permute-start(bf16[4,8192]{1,0:T(4,128)(2,1)S(1)} %shard_map.30.after_ref.own_ref.rest_0_), channel_id=1, source_target_pairs={{0,4},{1,5},{2,6},{3,7},{4,0},{5,1},{6,2},{7,3},{8,12},{9,13},{10,... | collective-permute-start | bytes 196616 | tf_op jit(solution)/shard_map/ppermute | solution.py:197
  17.1 1.2 %shard_map.31.by_pixel_ref = bf16[8192,208]{1,0:T(8,128)(2,1)S(1)} custom-call(bf16[208,8192]{1,0:T(8,128)(2,1)S(1)} %get-tuple-element.21.onehot_ref, bf16[4,8192]{1,0:T(4,128)(2,1)S(1)} %shard_map.30.after_ref.own_ref.rest_0_), custom_call_target="tpu_custom_call" | custom-call | flops 872415232 | bytes 6881280 | tf_op jit(solution)/shard_map/pallas_call | solution.py:183
  18.3 0.6 %collective-permute-done.3.rest_1_ = bf16[4,8192]{1,0:T(4,128)(2,1)S(1)} collective-permute-done((bf16[4,8192]{1,0:T(4,128)(2,1)S(1)}, bf16[4,8192]{1,0:T(4,128)(2,1)S(1)}, u32[]{:S(2)}, u32[]{:S(2)}) %collective-permute-start.3) | collective-permute-done | bytes 65568 | tf_op jit(solution)/shard_map/ppermute | solution.py:197
  18.9 1.7 %collective-permute-done.4.rest_2_ = bf16[4,8192]{1,0:T(4,128)(2,1)S(1)} collective-permute-done((bf16[4,8192]{1,0:T(4,128)(2,1)S(1)}, bf16[4,8192]{1,0:T(4,128)(2,1)S(1)}, u32[]{:S(2)}, u32[]{:S(2)}) %collective-permute-start.4) | collective-permute-done | bytes 65568 | tf_op jit(solution)/shard_map/ppermute | solution.py:197
  20.6 0.5 %collective-permute-start.6 = (bf16[4,8192]{1,0:T(4,128)(2,1)S(1)}, bf16[4,8192]{1,0:T(4,128)(2,1)S(1)}, u32[]{:S(2)}, u32[]{:S(2)}) collective-permute-start(bf16[4,8192]{1,0:T(4,128)(2,1)S(1)} %shard_map.30.after_ref.own_ref.rest_0_), channel_id=1, source_target_pairs={{0,1},{1,0},{2,3},{3,2},{4,5},{5,4},{6,7},{7,6},{8,9},{9,8},{10,11... | collective-permute-start | bytes 196616 | tf_op jit(solution)/shard_map/ppermute | solution.py:197
  21.1 0.4 %collective-permute-done.5.rest_3_ = bf16[4,8192]{1,0:T(4,128)(2,1)S(1)} collective-permute-done((bf16[4,8192]{1,0:T(4,128)(2,1)S(1)}, bf16[4,8192]{1,0:T(4,128)(2,1)S(1)}, u32[]{:S(2)}, u32[]{:S(2)}) %collective-permute-start.5) | collective-permute-done | bytes 65568 | tf_op jit(solution)/shard_map/ppermute | solution.py:197
  21.6 0.7 %shard_map.32.first_ref = f32[64,208]{1,0:T(8,128)S(1)} custom-call(bf16[8192,208]{1,0:T(8,128)(2,1)S(1)} %shard_map.31.by_pixel_ref, bf16[4,8192]{1,0:T(4,128)(2,1)S(1)} %shard_map.30.after_ref.own_ref.rest_0_, bf16[4,8192]{1,0:T(4,128)(2,1)S(1)} %shard_map.30.after_ref.own_ref.rest_0_, bf16[4,8192]{1,0:T(4,128)(2,1)S(1)} %collective-permute-done.3.rest_1_, ...), custom_call_target="tpu_custom_call" | custom-call | flops 872415232 | bytes 3788800 | tf_op jit(solution)/shard_map/pallas_call | solution.py:183
  22.4 0.3 %collective-permute-done.9.rest_3_ = bf16[4,8192]{1,0:T(4,128)(2,1)S(1)} collective-permute-done((bf16[4,8192]{1,0:T(4,128)(2,1)S(1)}, bf16[4,8192]{1,0:T(4,128)(2,1)S(1)}, u32[]{:S(2)}, u32[]{:S(2)}) %collective-permute-start.9) | collective-permute-done | bytes 65568 | tf_op jit(solution)/shard_map/ppermute | solution.py:197
  22.8 0.8 %shard_map.33 = (f32[50,128]{1,0:T(8,128)S(1)}, f32[50,128]{1,0:T(8,128)S(1)}, f32[50,128]{1,0:T(8,128)S(1)}, f32[50,128]{1,0:T(8,128)S(1)}) custom-call(bf16[8192,208]{1,0:T(8,128)(2,1)S(1)} %shard_map.31.by_pixel_ref, bf16[4,8192]{1,0:T(4,128)(2,1)S(1)} %shard_map.30.after_ref.own_ref.rest_0_, f32[64,208]{1,0:T(8,128)S(1)} %shard_map.32.first_ref, ...), custom_call_target="tpu_custom_call" | custom-call | flops 872415232 | bytes 3891200 | tf_op jit(solution)/shard_map/pallas_call | solution.py:183
  23.6 1.6 %collective-permute-start.10 = (f32[50,128]{1,0:T(8,128)S(1)}, f32[50,128]{1,0:T(8,128)S(1)}, u32[]{:S(2)}, u32[]{:S(2)}) collective-permute-start(f32[50,128]{1,0:T(8,128)S(1)} %get-tuple-element.28), channel_id=1, source_target_pairs={{0,24},{8,16},{16,8},{24,0},{1,25},{9,17},{17,9},{25,1},{2,26},{10... | collective-permute-start | bytes 76808 | tf_op jit(solution)/shard_map/ppermute | solution.py:197
  25.2 0.5 %collective-permute-start.11 = (f32[50,128]{1,0:T(8,128)S(1)}, f32[50,128]{1,0:T(8,128)S(1)}, u32[]{:S(2)}, u32[]{:S(2)}) collective-permute-start(f32[50,128]{1,0:T(8,128)S(1)} %get-tuple-element.29), channel_id=1, source_target_pairs={{0,16},{8,24},{16,0},{24,8},{1,17},{9,25},{17,1},{25,9},{2,18},{10... | collective-permute-start | bytes 76808 | tf_op jit(solution)/shard_map/ppermute | solution.py:197
  25.7 1.5 %collective-permute-start.12 = (f32[50,128]{1,0:T(8,128)S(1)}, f32[50,128]{1,0:T(8,128)S(1)}, u32[]{:S(2)}, u32[]{:S(2)}) collective-permute-start(f32[50,128]{1,0:T(8,128)S(1)} %get-tuple-element.30), channel_id=1, source_target_pairs={{0,8},{8,0},{16,24},{24,16},{1,9},{9,1},{17,25},{25,17},{2,10},{10... | collective-permute-start | bytes 76808 | tf_op jit(solution)/shard_map/ppermute | solution.py:197
  27.2 1.3 %collective-permute-done.10.rest_1_ = f32[50,128]{1,0:T(8,128)S(1)} collective-permute-done((f32[50,128]{1,0:T(8,128)S(1)}, f32[50,128]{1,0:T(8,128)S(1)}, u32[]{:S(2)}, u32[]{:S(2)}) %collective-permute-start.10) | collective-permute-done | bytes 25632 | tf_op jit(solution)/shard_map/ppermute | solution.py:197
  28.4 0.6 %collective-permute-done.11.rest_2_ = f32[50,128]{1,0:T(8,128)S(1)} collective-permute-done((f32[50,128]{1,0:T(8,128)S(1)}, f32[50,128]{1,0:T(8,128)S(1)}, u32[]{:S(2)}, u32[]{:S(2)}) %collective-permute-start.11) | collective-permute-done | bytes 25632 | tf_op jit(solution)/shard_map/ppermute | solution.py:197
  29.0 0.5 %collective-permute-done.12.rest_3_ = f32[50,128]{1,0:T(8,128)S(1)} collective-permute-done((f32[50,128]{1,0:T(8,128)S(1)}, f32[50,128]{1,0:T(8,128)S(1)}, u32[]{:S(2)}, u32[]{:S(2)}) %collective-permute-start.12) | collective-permute-done | bytes 25632 | tf_op jit(solution)/shard_map/ppermute | solution.py:197
  29.5 0.8 %shard_map.34 = f32[128,50]{1,0:T(8,128)} custom-call(f32[208,128]{1,0:T(8,128)S(1)} %get-tuple-element.20.counts_ref, f32[50,128]{1,0:T(8,128)S(1)} %get-tuple-element.27.rest_0_, f32[50,128]{1,0:T(8,128)S(1)} %collective-permute-done.10.rest_1_, f32[50,128]{1,0:T(8,128)S(1)} %collective-permute-done.11.rest_2_, f32[50,128]{1,0:T(8,128)S(1)} %collective-permute-done.12.rest_3_), custom_call_target="tpu_custom_call" | custom-call | flops 13631488 | bytes 234496 | tf_op jit(solution)/shard_map/pallas_call | solution.py:183
  (13 shorter events, 0.3 us)
Async XLA Ops:
  2.8 6.6 %collective-permute-start.2 = (f16[200,128]{1,0:T(8,128)(2,1)S(1)}, f16[200,128]{1,0:T(8,128)(2,1)S(1)}, u32[]{:S(2)}, u32[]{:S(2)}) collective-permute-start(f16[200,128]{1,0:T(8,128)(2,1)S(1)} %multiply_convert_fusion), channel_id=1, source_target_pairs={{0,24},{8,16},{16,8},{24,0},{1,25},{9,17},{17,9},{25,1},{2,26},{10... | collective-permute-start | bytes 153608 | tf_op jit(solution)/shard_map/ppermute | solution.py:197
  6.7 4.1 %collective-permute-start.1 = (f16[200,128]{1,0:T(8,128)(2,1)S(1)}, f16[200,128]{1,0:T(8,128)(2,1)S(1)}, u32[]{:S(2)}, u32[]{:S(2)}) collective-permute-start(f16[200,128]{1,0:T(8,128)(2,1)S(1)} %multiply_convert_fusion), channel_id=1, source_target_pairs={{0,16},{8,24},{16,0},{24,8},{1,17},{9,25},{17,1},{25,9},{2,18},{10... | collective-permute-start | bytes 153608 | tf_op jit(solution)/shard_map/ppermute | solution.py:197
  7.2 4.1 %collective-permute-start = (f16[200,128]{1,0:T(8,128)(2,1)S(1)}, f16[200,128]{1,0:T(8,128)(2,1)S(1)}, u32[]{:S(2)}, u32[]{:S(2)}) collective-permute-start(f16[200,128]{1,0:T(8,128)(2,1)S(1)} %multiply_convert_fusion), channel_id=1, source_target_pairs={{0,8},{8,0},{16,24},{24,16},{1,9},{9,1},{17,25},{25,17},{2,10},{10... | collective-permute-start | bytes 153608 | tf_op jit(solution)/shard_map/ppermute | solution.py:197
  12.7 6.2 %collective-permute-start.3 = (bf16[4,8192]{1,0:T(4,128)(2,1)S(1)}, bf16[4,8192]{1,0:T(4,128)(2,1)S(1)}, u32[]{:S(2)}, u32[]{:S(2)}) collective-permute-start(bf16[4,8192]{1,0:T(4,128)(2,1)S(1)} %shard_map.30.after_ref.own_ref.rest_0_), channel_id=1, source_target_pairs={{0,6},{1,7},{2,4},{3,5},{4,2},{5,3},{6,0},{7,1},{8,14},{9,15},{10,... | collective-permute-start | bytes 196616 | tf_op jit(solution)/shard_map/ppermute | solution.py:197
  16.3 4.3 %collective-permute-start.4 = (bf16[4,8192]{1,0:T(4,128)(2,1)S(1)}, bf16[4,8192]{1,0:T(4,128)(2,1)S(1)}, u32[]{:S(2)}, u32[]{:S(2)}) collective-permute-start(bf16[4,8192]{1,0:T(4,128)(2,1)S(1)} %shard_map.30.after_ref.own_ref.rest_0_), channel_id=1, source_target_pairs={{0,2},{1,3},{2,0},{3,1},{4,6},{5,7},{6,4},{7,5},{8,10},{9,11},{10,... | collective-permute-start | bytes 196616 | tf_op jit(solution)/shard_map/ppermute | solution.py:197
  16.4 5.2 %collective-permute-start.5 = (bf16[4,8192]{1,0:T(4,128)(2,1)S(1)}, bf16[4,8192]{1,0:T(4,128)(2,1)S(1)}, u32[]{:S(2)}, u32[]{:S(2)}) collective-permute-start(bf16[4,8192]{1,0:T(4,128)(2,1)S(1)} %shard_map.30.after_ref.own_ref.rest_0_), channel_id=1, source_target_pairs={{0,4},{1,5},{2,6},{3,7},{4,0},{5,1},{6,2},{7,3},{8,12},{9,13},{10,... | collective-permute-start | bytes 196616 | tf_op jit(solution)/shard_map/ppermute | solution.py:197
  20.6 1.8 %collective-permute-start.7 = (bf16[4,8192]{1,0:T(4,128)(2,1)S(1)}, bf16[4,8192]{1,0:T(4,128)(2,1)S(1)}, u32[]{:S(2)}, u32[]{:S(2)}) collective-permute-start(bf16[4,8192]{1,0:T(4,128)(2,1)S(1)} %collective-permute-done.3.rest_1_), channel_id=1, source_target_pairs={{0,1},{1,0},{2,3},{3,2},{4,5},{5,4},{6,7},{7,6},{8,9},{9,8},{10,11... | collective-permute-start | bytes 196616 | tf_op jit(solution)/shard_map/ppermute | solution.py:197
  20.6 1.8 %collective-permute-start.6 = (bf16[4,8192]{1,0:T(4,128)(2,1)S(1)}, bf16[4,8192]{1,0:T(4,128)(2,1)S(1)}, u32[]{:S(2)}, u32[]{:S(2)}) collective-permute-start(bf16[4,8192]{1,0:T(4,128)(2,1)S(1)} %shard_map.30.after_ref.own_ref.rest_0_), channel_id=1, source_target_pairs={{0,1},{1,0},{2,3},{3,2},{4,5},{5,4},{6,7},{7,6},{8,9},{9,8},{10,11... | collective-permute-start | bytes 196616 | tf_op jit(solution)/shard_map/ppermute | solution.py:197
  21.1 1.3 %collective-permute-start.8 = (bf16[4,8192]{1,0:T(4,128)(2,1)S(1)}, bf16[4,8192]{1,0:T(4,128)(2,1)S(1)}, u32[]{:S(2)}, u32[]{:S(2)}) collective-permute-start(bf16[4,8192]{1,0:T(4,128)(2,1)S(1)} %collective-permute-done.4.rest_2_), channel_id=1, source_target_pairs={{0,1},{1,0},{2,3},{3,2},{4,5},{5,4},{6,7},{7,6},{8,9},{9,8},{10,11... | collective-permute-start | bytes 196616 | tf_op jit(solution)/shard_map/ppermute | solution.py:197
  21.5 1.3 %collective-permute-start.9 = (bf16[4,8192]{1,0:T(4,128)(2,1)S(1)}, bf16[4,8192]{1,0:T(4,128)(2,1)S(1)}, u32[]{:S(2)}, u32[]{:S(2)}) collective-permute-start(bf16[4,8192]{1,0:T(4,128)(2,1)S(1)} %collective-permute-done.5.rest_3_), channel_id=1, source_target_pairs={{0,1},{1,0},{2,3},{3,2},{4,5},{5,4},{6,7},{7,6},{8,9},{9,8},{10,11... | collective-permute-start | bytes 196616 | tf_op jit(solution)/shard_map/ppermute | solution.py:197
  23.6 4.8 %collective-permute-start.10 = (f32[50,128]{1,0:T(8,128)S(1)}, f32[50,128]{1,0:T(8,128)S(1)}, u32[]{:S(2)}, u32[]{:S(2)}) collective-permute-start(f32[50,128]{1,0:T(8,128)S(1)} %get-tuple-element.28), channel_id=1, source_target_pairs={{0,24},{8,16},{16,8},{24,0},{1,25},{9,17},{17,9},{25,1},{2,26},{10... | collective-permute-start | bytes 76808 | tf_op jit(solution)/shard_map/ppermute | solution.py:197
  25.2 3.9 %collective-permute-start.11 = (f32[50,128]{1,0:T(8,128)S(1)}, f32[50,128]{1,0:T(8,128)S(1)}, u32[]{:S(2)}, u32[]{:S(2)}) collective-permute-start(f32[50,128]{1,0:T(8,128)S(1)} %get-tuple-element.29), channel_id=1, source_target_pairs={{0,16},{8,24},{16,0},{24,8},{1,17},{9,25},{17,1},{25,9},{2,18},{10... | collective-permute-start | bytes 76808 | tf_op jit(solution)/shard_map/ppermute | solution.py:197
  25.7 3.9 %collective-permute-start.12 = (f32[50,128]{1,0:T(8,128)S(1)}, f32[50,128]{1,0:T(8,128)S(1)}, u32[]{:S(2)}, u32[]{:S(2)}) collective-permute-start(f32[50,128]{1,0:T(8,128)S(1)} %get-tuple-element.30), channel_id=1, source_target_pairs={{0,8},{8,0},{16,24},{24,16},{1,9},{9,1},{17,25},{25,17},{2,10},{10... | collective-permute-start | bytes 76808 | tf_op jit(solution)/shard_map/ppermute | solution.py:197
